TPU v7x, 256 devices: a whole 4x4x8 slice. The times are simulated.
256 devices in a mesh: gx: 16 (over x, y_lo, core), gy: 16 (over y_hi, z).
Axes of the slice: x: 4, y: 4 (y_hi: 2, y_lo: 2; y = y_hi * 2 + y_lo), z: 8, core: 2. Of those that a mesh axis runs over, the one named last changes fastest.
Arguments:
- object_field: float32 [2, 1024, 1024], P(None, 'gy', 'gx'), may hold values from -1 to 1
- probe_modes: float32 [2, 1024, 128], P(None, ('gy', 'gx')), may hold values from -1.5 to 1.5
- positions: int32 [16, 16, 12, 2], P('gy', 'gx'), may hold values from 4 to 60, as said below
- amplitudes: float32 [16, 16, 12, 128, 128], P('gy', 'gx'), may hold values from 0 to 2
Outputs:
- object_out: float32 [2, 1024, 1024], P(None, 'gy', 'gx')
- probe_out: float32 [2, 1024, 128], P(None, ('gy', 'gx'))
Inputs may be any that keep to these rules, and one draw needn't show every extreme that they name: `positions`: each entry is a (row, column) inside its own tile; the centres of one tile lie at distinct cells of the 16 grid, each moved from the cell's middle by at most 4 cells along each dimension.
All inputs are finite; a program needn't handle non-finite values.
Results may differ from a plain program's by a relative error of at most 0.00065.
The roundings to bfloat16 on the way count: a program that leaves them out, or rounds other values in their place, can miss the bound.
Values sent between devices are 32-bit elements; how exact they have to be, the bound alone decides.
No kernel may reach another device: no remote copies, remote signals or barrier semaphores. Data moves between devices by JAX's collectives and lax.ppermute only.
A program may use at most 64 MiB of HBM per device.

v0:
```python
import math

import jax
import jax.numpy as jnp
from jax import lax
from jax.sharding import PartitionSpec as P

MODES = 8
ITERS = 2


SOFT_FLOOR = 0.05
OBJECT_REG = 1.0
PROBE_REG = 1.0


def from_behind(block, axis, distance):
    devices = range(lax.axis_size(axis))
    route = [(i - distance, i) for i in devices if i - distance in devices]
    return lax.ppermute(block, axis, route)


def extended_2(array, sides, width):
    for axis, dim in sides:
        peers, length = (lax.axis_size(axis), array.shape[dim])
        up = [(i, (i + 1) % peers) for i in range(peers - 1)]
        down = [(j, i) for i, j in up]
        last = lax.slice_in_dim(array, length - width, length, axis=dim)
        initial = lax.slice_in_dim(array, 0, width, axis=dim)
        before = lax.ppermute(last, axis, up)
        after = lax.ppermute(initial, axis, down)
        array = jnp.concatenate([before, array, after], axis=dim)
    return array


def tables(probe_side, sign_flip):
    indices = jnp.arange(probe_side, dtype=jnp.int32)
    phases = indices[:, None] * indices[None, :] % probe_side
    angles = phases.astype(jnp.float32) * (2.0 * math.pi / probe_side)
    factor = 1.0 / math.sqrt(probe_side)
    cosine = jnp.cos(angles) * factor
    sine_part = sign_flip * jnp.sin(angles) * factor
    left_op = jnp.stack(
        [jnp.stack([cosine, -sine_part]), jnp.stack([sine_part, cosine])]
    ).transpose(0, 2, 1, 3)
    right_op = jnp.stack(
        [jnp.stack([cosine, sine_part]), jnp.stack([-sine_part, cosine])]
    ).transpose(0, 2, 1, 3)
    return (left_op.astype(jnp.bfloat16), right_op.astype(jnp.bfloat16))


def transform(signal, operators):
    left_op, right_op = operators
    halfway = jnp.einsum(
        "dpcr,crmq->dpmq", left_op, signal, preferred_element_type=jnp.float32
    ).astype(jnp.bfloat16)
    return jnp.einsum("crmq,cqdk->drmk", halfway, right_op, preferred_element_type=jnp.float32)


def position_terms(patch_obj, probe, measured, forward, inverse):
    obj_real = patch_obj[0][:, None, :]
    obj_imag = patch_obj[1][:, None, :]
    wave_real = probe[0] * obj_real - probe[1] * obj_imag
    wave_imag = probe[0] * obj_imag + probe[1] * obj_real
    signal = jnp.stack([wave_real, wave_imag]).astype(jnp.bfloat16)
    spectrum = transform(signal, forward)
    intensity = jnp.sum(spectrum[0] * spectrum[0] + spectrum[1] * spectrum[1], axis=1)
    shrink = 1.0 - measured / jnp.sqrt(intensity + SOFT_FLOOR)
    residual = (spectrum * shrink[None, :, None, :]).astype(jnp.bfloat16)
    change = transform(residual, inverse)
    grad_real = jnp.sum(probe[0] * change[0] + probe[1] * change[1], axis=1)
    grad_imag = jnp.sum(probe[0] * change[1] - probe[1] * change[0], axis=1)
    probe_real = obj_real * change[0] + obj_imag * change[1]
    probe_imag = obj_real * change[1] - obj_imag * change[0]
    weight_probe = patch_obj[0] * patch_obj[0] + patch_obj[1] * patch_obj[1]
    return (jnp.stack([grad_real, grad_imag]), jnp.stack([probe_real, probe_imag]), weight_probe)


def fold_rows(gradient, margin, tile_side):
    extent = gradient.shape[1]
    for direction in (1, -1):
        rim_part = gradient[:, extent - margin :, :] if direction == 1 else gradient[:, :margin, :]
        offset = margin if direction == 1 else tile_side
        arrived = from_behind(rim_part, "gy", direction)
        gradient = gradient.at[:, offset : offset + margin, :].add(arrived)
    return gradient[:, margin : margin + tile_side, :]


def fold_cols(gradient, margin, tile_side):
    extent = gradient.shape[2]
    for direction in (1, -1):
        rim_part = gradient[:, :, extent - margin :] if direction == 1 else gradient[:, :, :margin]
        offset = margin if direction == 1 else tile_side
        arrived = from_behind(rim_part, "gx", direction)
        gradient = gradient.at[:, :, offset : offset + margin].add(arrived)
    return gradient[:, :, margin : margin + tile_side]


def unpack_probe(probe_rows, probe_side):
    return probe_rows.reshape(2, MODES, probe_side, probe_side).transpose(0, 2, 1, 3)


def local(object_field, probe_modes, positions, amplitudes):
    probe_side = amplitudes.shape[-1]
    margin = probe_side // 2
    tile_side = object_field.shape[1]
    centres = positions.reshape(-1, 2)
    measured_all = amplitudes.reshape(-1, probe_side, probe_side)
    forward = tables(probe_side, -1.0)
    inverse = tables(probe_side, 1.0)
    gathered = lax.all_gather(probe_modes, ("gy", "gx"), axis=1, tiled=True)
    probe = unpack_probe(gathered, probe_side)
    own_rows = probe_modes
    current = object_field
    for iteration in range(ITERS):
        extended = extended_2(current, (("gy", 1), ("gx", 2)), margin)
        weight_obj = jnp.sum(probe[0] * probe[0] + probe[1] * probe[1], axis=1)

        def visit(running, visit_item):
            grad_obj, grad_probe, weight_probe = running
            row_at, col_at, measured = visit_item
            zero_index = jnp.int32(0)
            patch_obj = lax.dynamic_slice(
                extended, (zero_index, row_at, col_at), (2, probe_side, probe_side)
            )
            g_obj, g_probe, w_probe = position_terms(patch_obj, probe, measured, forward, inverse)
            stacked = jnp.concatenate([g_obj, weight_obj[None]], axis=0)
            before = lax.dynamic_slice(
                grad_obj, (zero_index, row_at, col_at), (3, probe_side, probe_side)
            )
            grad_obj = lax.dynamic_update_slice(
                grad_obj, before + stacked, (zero_index, row_at, col_at)
            )
            return ((grad_obj, grad_probe + g_probe, weight_probe + w_probe), None)

        initial = (
            jnp.zeros((3, tile_side + probe_side, tile_side + probe_side), jnp.float32),
            jnp.zeros((2, probe_side, MODES, probe_side), jnp.float32),
            jnp.zeros((probe_side, probe_side), jnp.float32),
        )
        (grad_obj, grad_probe, weight_probe), _ = lax.scan(
            visit, initial, (centres[:, 0], centres[:, 1], measured_all)
        )
        folded = fold_cols(fold_rows(grad_obj, margin, tile_side), margin, tile_side)
        new_object = current - folded[0:2] / (folded[2] + OBJECT_REG)
        grad_rows = grad_probe.transpose(0, 2, 1, 3).reshape(2, MODES * probe_side, probe_side)
        totals, weight_total = lax.psum((grad_rows, weight_probe), ("gy", "gx"))
        whole_probe = probe.transpose(0, 2, 1, 3)
        whole_probe = whole_probe - totals.reshape(2, MODES, probe_side, probe_side) / (
            weight_total[None, None] + PROBE_REG
        )
        whole_probe = whole_probe.reshape(2, MODES * probe_side, probe_side)
        probe = unpack_probe(whole_probe, probe_side)
        row_count = own_rows.shape[1]
        own_rows = lax.dynamic_slice_in_dim(
            whole_probe, lax.axis_index(("gy", "gx")) * row_count, row_count, 1
        )
        current = new_object
    return (current, own_rows)


def solution(mesh):
    return jax.shard_map(
        local,
        mesh=mesh,
        in_specs=(
            P(None, "gy", "gx"),
            P(None, ("gy", "gx"), None),
            P("gy", "gx", None, None),
            P("gy", "gx", None, None, None),
        ),
        out_specs=(P(None, "gy", "gx"), P(None, ("gy", "gx"), None)),
        check_vma=False,
    )
```

profile of v0, /device:TPU:16, one launch (start us, length us, event | category | flops | bytes accessed | tf_op | source)
XLA Modules:
  0.0 1355.3 jit_solution(5158283582343708737)
XLA Ops:
  8.6 3.8 collective-permute-start
  12.4 5.6 collective-permute-start.1
  24.8 3.6 collective-permute-done.3
  29.3 362.2 %all-gather.2.cloned.1.call-done = f32[2,1024,128]{2,0,1:T(2,128)} async-done(((f32[2,4,128]{2,0,1:T(2,128)}), f32[2,1024,128]{2,0,1:T(2,128)}) %all-gather.2.cloned.1.call-update) | async-done | bytes 1048592 | tf_op jit(solution)/shard_map/all_gather | solution.py:111
  394.4 205.2 %while.38 = (s32[]{:T(128)}, f32[3,192,192]{2,1,0:T(8,128)}, f32[2,128,8,128]{3,1,0,2:T(8,128)}, f32[128,128]{1,0:T(8,128)}, s32[12]{0:T(128)S(1)}, /*index=5*/s...) while((s32[]{:T(128)}, f32[3,192,192]{2,1,0:T(8,128)}, ...), condition=%wide.region_5.6_spmd.clone, body=%wide.region_1.5_spmd.clone.sunk | while | flops 543391744 | bytes 27918840 | solution.py:141
  442.1 2.9 dynamic_update_slice.10
  459.3 2.8 dynamic_update_slice.10
  510.6 2.9 dynamic_update_slice.10
  544.8 2.8 dynamic_update_slice.10
  600.7 2.8 collective-permute-start.4
  603.6 6.7 collective-permute-start.5
  610.2 2.8 collective-permute-done.4
  623.2 7.5 collective-permute-start.9
  632.6 4.2 collective-permute-start.10
  638.1 3.2 collective-permute-done.11
  642.3 236.7 %all-reduce.7.cloned.1.call-done = (f32[2,1024,128]{2,0,1:T(2,128)}, f32[128,128]{1,0:T(8,128)}) async-done(((f32[2,1024,128]{2,0,1:T(2,128)}, f32[128,128]{1,0:T(8,128)}), (f32[2,1024,128]{2,0,1:T(2,128)}, f32[128,128]{1,0:T(8,128)})) %all-reduce.7.cloned.1.call-update) | async-done | bytes 1114128 | tf_op jit(solution)/shard_map/psum | solution.py:147
  882.9 197.0 %while.39 = (s32[]{:T(128)}, f32[3,192,192]{2,1,0:T(8,128)}, f32[2,128,8,128]{3,1,0,2:T(8,128)}, f32[128,128]{1,0:T(8,128)}, s32[12]{0:T(128)S(1)}, /*index=5*/s...) while((s32[]{:T(128)}, f32[3,192,192]{2,1,0:T(8,128)}, ...), condition=%wide.region_13.14_spmd.clone, body=%wide.region_9.13_spmd.clone.sunk | while | flops 543391744 | bytes 27918840 | solution.py:141
  928.5 2.9 dynamic_update_slice.11
  945.0 2.8 dynamic_update_slice.11
  994.2 2.9 dynamic_update_slice.11
  1027.1 2.8 dynamic_update_slice.11
  1082.9 7.5 collective-permute-start.13
  1090.4 3.0 copy.30
  1101.5 245.1 %all-reduce.5.cloned.1.call-done = (f32[2,1024,128]{2,0,1:T(2,128)}, f32[128,128]{1,0:T(8,128)}) async-done(((f32[2,1024,128]{2,0,1:T(2,128)}, f32[128,128]{1,0:T(8,128)}), (f32[2,1024,128]{2,0,1:T(2,128)}, f32[128,128]{1,0:T(8,128)})) %all-reduce.5.cloned.1.call-update) | async-done | bytes 1114128 | tf_op jit(solution)/shard_map/psum | solution.py:147
  (713 shorter events, 335.5 us)
Async XLA Ops:
  7.2 384.3 %all-gather.2.cloned.1.call-start = ((), (), s32[]{:S(2)}) async-start(), calls=%async_computation | async-start | bytes 1052672 | tf_op jit(solution)/shard_map/all_gather | solution.py:111
  8.5 870.5 %all-reduce.7.cloned.1.call-start = ((), (), s32[]{:S(2)}) async-start(), calls=%async_computation.2 | async-start | bytes 2228224 | tf_op jit(solution)/shard_map/psum | solution.py:147
  8.6 11.9 collective-permute-start
  12.4 8.9 collective-permute-start.1
  21.4 3.5 collective-permute-start.2
  22.8 5.6 collective-permute-start.3
  441.3 3.7 copy-start.1
  509.7 3.7 copy-start.1
  599.6 18.2 %copy-start.2 = (f32[2,128,8,128]{3,1,0,2:T(8,128)S(1)}, f32[2,128,8,128]{3,1,0,2:T(8,128)}, u32[]{:S(2)}) copy-start(f32[2,128,8,128]{3,1,0,2:T(8,128)} %get-tuple-element.247) | copy-start | bytes 3145732
  600.7 12.3 collective-permute-start.4
  603.6 10.7 collective-permute-start.5
  615.2 4.5 collective-permute-start.6
  616.5 4.6 collective-permute-start.7
  619.7 260.2 %copy-start.13 = (f32[2,1024,128]{2,0,1:T(2,128)S(1)}, f32[2,1024,128]{2,0,1:T(2,128)}, u32[]{:S(2)}) copy-start(f32[2,1024,128]{2,0,1:T(2,128)} %all-gather.2.cloned.1.call-done) | copy-start | bytes 3145732
  619.7 726.9 %all-reduce.5.cloned.1.call-start = ((), (), s32[]{:S(2)}) async-start(), calls=%async_computation.1 | async-start | bytes 2228224 | tf_op jit(solution)/shard_map/psum | solution.py:147
  621.2 20.1 %copy-start.16 = (f32[2,64,64]{2,1,0:T(8,128)}, f32[2,64,64]{2,1,0:T(8,128)S(1)}, u32[]{:S(2)}) copy-start(f32[2,64,64]{2,1,0:T(8,128)S(1)} %fusion.68) | copy-start | bytes 98308
  621.2 9.8 collective-permute-start.8
  623.2 9.4 collective-permute-start.9
  632.6 5.5 collective-permute-start.10
  636.8 4.5 collective-permute-start.11
  1080.9 12.5 collective-permute-start.12
  1082.9 10.7 collective-permute-start.13
  1094.6 2.7 collective-permute-start.14
  1095.9 4.1 collective-permute-start.15
  (172 other events, 220.1 us)
Sparse Core Ops, SparseCore 0:
  10.4 381.0 all-gather.1
  619.8 259.1 all-reduce.6
  1093.6 252.9 all-reduce.4
where the time goes:
time: 1360 us
  waiting for transfers between devices  861 us (63%)
  local copies, waits for them, and re-layouts  158 us (12%)
  other arithmetic  136 us (10%)
  loops' own time  88.1 us (6%)
  starting transfers between devices  51.3 us (4%)
  matrix products  46.9 us (3%)
  between operations  14.2 us (1%)
    psum x2, waiting for transfers between devices, local(): totals, weight_total = lax.psum((grad_rows, weight_probe), ('gy', 'gx'))  482 us
    all_gather x1, waiting for transfers between devices, local(): gathered = lax.all_gather(probe_modes, ('gy', 'gx'), axis=1, tiled=True)  362 us
    another operation x2, loops' own time, local(): lax.scan(visit, initial, (centres[:, 0], centres[:, 1], measured_all))  88.1 us
    dynamic_update_slice x24, local copies, waits for them, and re-layouts, visit(): lax.dynamic_update_slice(grad_obj, before + stacked, (zero_index, row_at,...  66.4 us
    add x48, other arithmetic, visit(): return ((grad_obj, grad_probe + g_probe, weight_probe + w_probe), None)  50.6 us
    while x336, local copies, waits for them, and re-layouts  49.5 us
    dot_general x48, matrix products, transform(): jnp.einsum('crmq,cqdk->drmk', halfway, right_op, preferred_element_type=j...  46.9 us
    sub x24, other arithmetic, position_terms(): shrink = 1.0 - measured / jnp.sqrt(intensity + SOFT_FLOOR)  35.8 us
  transfers between devices with their start and end apart: 19, of which 12 were waited for; matrix products, arithmetic and copies ran while one was open for 1% of the time, Pallas kernels for 0%

commit v1 on v0

v1 whole, which is shorter than its diff:
```python
import math

import jax
import jax.numpy as jnp
import numpy as np
from jax import lax
from jax.experimental import pallas as pl
from jax.experimental.pallas import tpu as pltpu
from jax.sharding import PartitionSpec as P

MODES = 8
ITERS = 2
SOFT_FLOOR = 0.05
OBJECT_REG = 1.0
PROBE_REG = 1.0

BAND = 32
DEVICES = 256
CORE = 1
Y_FAR, Y_NEAR = 0b10000010, 0b00000010
X_FAR, X_NEAR = 0b00001100, 0b00000100
Z_STEPS = (0b00010000, 0b00100000, 0b01100000)
PLANE_STEPS = ((Y_FAR, X_FAR), (Y_NEAR, X_NEAR), (X_FAR, Y_FAR), (X_NEAR, Y_NEAR))


def mesh_place(device):
    return (device % 16) * 16 + device // 16


def exchange(block, flips):
    if isinstance(flips, int):
        flips = (flips, flips)
    pairs = [(d, d ^ flips[d & 1]) for d in range(DEVICES)]
    return lax.ppermute(block, ("gx", "gy"), [(mesh_place(a), mesh_place(b)) for a, b in pairs])


def table(side):
    index = np.arange(side)
    angle = (index[:, None] * index[None, :] % side).astype(np.float32) * np.float32(2.0 * math.pi / side)
    factor = np.float32(1.0 / math.sqrt(side))
    real = (np.cos(angle) * factor).astype(jnp.bfloat16)
    imag = (-np.sin(angle) * factor).astype(jnp.bfloat16)
    return np.block([[real, -imag], [imag, real]])


def aligned(row):
    return pl.multiple_of(row - lax.rem(row, 8), 8)


def gray(delta):
    return lax.bitwise_xor(delta, lax.shift_right_logical(delta, 1))


def groups(spot_ref):
    for x in range(4):
        for y in range(4):
            far_x, far_y = gray(lax.bitwise_xor(spot_ref[1], x)), gray(lax.bitwise_xor(spot_ref[2], y))
            yield (y // 2) * 64 + x * 2 + y % 2, far_y * 4 + far_x, far_x * 4 + far_y


def sweep_kernel(
    pos_ref, spot_ref, ext_ref, mine_ref, other_ref, amp_ref, a_ref, b_ref,
    keep_ref, send_ref, top_ref, middle_ref, bottom_ref,
    probe_s, grad_s, obj_s, wp_s, patch_s, weight_s, half_s, miss_s, back_s,
):
    count, side = amp_ref.shape[0], amp_ref.shape[1]
    bands = side // BAND
    wide = 2 * side
    on_zero = spot_ref[0] == 0
    upper = lax.broadcasted_iota(jnp.int32, (8, side), 0) < 4

    def joined(first, second):
        return jnp.where(upper, first, pltpu.roll(second, 4, 0)), jnp.where(upper, pltpu.roll(first, 4, 0), second)

    for pair, place_0, place_1 in groups(spot_ref):
        for z in range(8):
            tile_0 = jnp.where(on_zero, mine_ref[place_0, z], other_ref[place_0, z])
            tile_1 = jnp.where(on_zero, other_ref[place_1, z], mine_ref[place_1, z])
            rows = pl.ds((pair + z * 8) * 8, 8)
            probe_s[0, rows, :], probe_s[1, rows, :] = joined(tile_0, tile_1)

    obj_s[...] = jnp.zeros_like(obj_s)
    grad_s[...] = jnp.zeros_like(grad_s)
    wp_s[...] = jnp.zeros_like(wp_s)
    weight = jnp.zeros((side, side), jnp.float32)
    for m in range(MODES):
        for c in range(2):
            p = probe_s[c, pl.ds(m * side, side), :]
            weight = weight + p * p
    weight_s[...] = weight

    def fetch(i, slot):
        row, col = pos_ref[i, 0], pos_ref[i, 1]
        for c in range(2):
            rows = ext_ref[c, pl.ds(aligned(row), side + 8), :]
            rows = pltpu.roll(rows, wide - col, 1)[:, :side]
            patch_s[slot, c] = pltpu.roll(rows, side + 8 - lax.rem(row, 8), 0)[:side]
        wp_s[...] += patch_s[slot, 0] * patch_s[slot, 0] + patch_s[slot, 1] * patch_s[slot, 1]

    def forward_rows(slot, j):
        real, imag = [], []
        for m in (2 * j, 2 * j + 1):
            p_re = probe_s[0, pl.ds(m * side, side), :]
            p_im = probe_s[1, pl.ds(m * side, side), :]
            o_re, o_im = patch_s[slot, 0], patch_s[slot, 1]
            real.append((p_re * o_re - p_im * o_im).astype(jnp.bfloat16))
            imag.append((p_re * o_im + p_im * o_re).astype(jnp.bfloat16))
        psi = jnp.concatenate([jnp.concatenate(real, 1), jnp.concatenate(imag, 1)], 0)
        half = jnp.dot(a_ref[...], psi, preferred_element_type=jnp.float32).astype(jnp.bfloat16)
        for k in range(2):
            lanes = slice(k * side, (k + 1) * side)
            half_s[2 * j + k] = jnp.concatenate([half[:side, lanes], half[side:, lanes]], 1)

    def forward_cols(i, b):
        rows = slice(b * BAND, (b + 1) * BAND)
        half = half_s[:, rows, :].reshape(MODES * BAND, wide)
        far = jnp.dot(half, b_ref[...], preferred_element_type=jnp.float32).reshape(MODES, BAND, wide)
        power = jnp.sum(far * far, axis=0)
        power = power[:, :side] + power[:, side:]
        shrink = 1.0 - amp_ref[i, rows, :] * lax.rsqrt(power + SOFT_FLOOR)
        shrink = jnp.concatenate([shrink, shrink], 1)
        for m in range(MODES):
            miss = (far[m] * shrink).astype(jnp.bfloat16)
            miss_s[pl.ds(b * BAND, BAND), pl.ds(m * side, side)] = miss[:, :side]
            miss_s[pl.ds(side + b * BAND, BAND), pl.ds(m * side, side)] = miss[:, side:]

    def inverse_rows(j):
        miss = miss_s[:, pl.ds(j * wide, wide)]
        back = jnp.dot(b_ref[...], miss, preferred_element_type=jnp.float32).astype(jnp.bfloat16)
        for k in range(2):
            lanes = slice(k * side, (k + 1) * side)
            back_s[2 * j + k] = jnp.concatenate([back[:side, lanes], back[side:, lanes]], 1)

    def inverse_cols(i, slot, b):
        row, col = pos_ref[i, 0], pos_ref[i, 1]
        rows = slice(b * BAND, (b + 1) * BAND)
        back = back_s[:, rows, :].reshape(MODES * BAND, wide)
        delta = jnp.dot(back, a_ref[...], preferred_element_type=jnp.float32).reshape(MODES, BAND, wide)
        o_re, o_im = patch_s[slot, 0, rows, :], patch_s[slot, 1, rows, :]
        g_re = jnp.zeros((BAND, side), jnp.float32)
        g_im = jnp.zeros((BAND, side), jnp.float32)
        for m in range(MODES):
            span = pl.ds(m * side + b * BAND, BAND)
            d_re, d_im = delta[m, :, :side], delta[m, :, side:]
            p_re, p_im = probe_s[0, span, :], probe_s[1, span, :]
            g_re += p_re * d_re + p_im * d_im
            g_im += p_re * d_im - p_im * d_re
            grad_s[0, span, :] += o_re * d_re + o_im * d_im
            grad_s[1, span, :] += o_re * d_im - o_im * d_re
        for c, part in enumerate((g_re, g_im, weight_s[rows, :])):
            part = jnp.concatenate([part, jnp.zeros((8, side), jnp.float32)], 0)
            part = pltpu.roll(part, lax.rem(row, 8), 0)
            placed = pltpu.roll(jnp.concatenate([part, jnp.zeros_like(part)], 1), col, 1)
            obj_s[c, pl.ds(aligned(row) + b * BAND, BAND + 8), :] += placed

    fetch(0, 0)
    for j in range(MODES // 2):
        forward_rows(0, j)
    for b in range(bands):
        forward_cols(0, b)

    def step(i, carry):
        slot = lax.rem(i, 2)
        fetch(i + 1, 1 - slot)
        for j in range(MODES // 2):
            inverse_rows(j)
            forward_rows(1 - slot, j)
        for b in range(bands):
            inverse_cols(i, slot, b)
            forward_cols(i + 1, b)
        return carry

    lax.fori_loop(0, count - 1, step, 0)
    last = count - 1
    for j in range(MODES // 2):
        inverse_rows(j)
    for b in range(bands):
        inverse_cols(last, last % 2, b)

    tile = side // 2
    top_ref[...] = obj_s[:, :tile, :]
    middle_ref[...] = obj_s[:, tile : 2 * tile, :]
    bottom_ref[...] = obj_s[:, 2 * tile :, :]
    for pair, place_0, place_1 in groups(spot_ref):
        place_mine = jnp.where(on_zero, place_0, place_1)
        place_other = jnp.where(on_zero, place_1, place_0)
        for slot in range(9):
            if slot < 8:
                rows = pl.ds((pair + slot * 8) * 8, 8)
                tile_0, tile_1 = joined(grad_s[0, rows, :], grad_s[1, rows, :])
            else:
                start = (pair % 8) * 8
                tile_0, tile_1 = joined(wp_s[pl.ds(start, 8), :], wp_s[pl.ds(start + side // 2, 8), :])
            keep_ref[place_mine, slot] = jnp.where(on_zero, tile_0, tile_1)
            send_ref[place_other, slot] = jnp.where(on_zero, tile_1, tile_0)


def sweep(centres, spot, extended, mine, other, measured, left_op, right_op):
    count, side = measured.shape[0], measured.shape[1]
    tile, wide, extent = side // 2, 2 * side, extended.shape[1]
    rows = MODES * side
    vmem = pl.BlockSpec(memory_space=pltpu.VMEM)
    smem = pl.BlockSpec(memory_space=pltpu.SMEM)
    f32, bf16 = jnp.float32, jnp.bfloat16
    half_sum = jax.ShapeDtypeStruct((16, 9, 8, side), f32)
    strip = jax.ShapeDtypeStruct((3, tile, wide), f32)
    return pl.pallas_call(
        sweep_kernel,
        in_specs=[smem, smem] + [vmem] * 6,
        out_specs=[vmem] * 5,
        out_shape=[half_sum, half_sum, strip, strip, strip],
        scratch_shapes=[
            pltpu.VMEM((2, rows, side), f32),
            pltpu.VMEM((2, rows, side), f32),
            pltpu.VMEM((3, extent, wide), f32),
            pltpu.VMEM((side, side), f32),
            pltpu.VMEM((2, 2, side, side), f32),
            pltpu.VMEM((side, side), f32),
            pltpu.VMEM((MODES, side, wide), bf16),
            pltpu.VMEM((wide, rows), bf16),
            pltpu.VMEM((MODES, side, wide), bf16),
        ],
        compiler_params=pltpu.CompilerParams(vmem_limit_bytes=32 << 20),
        cost_estimate=pl.CostEstimate(
            flops=count * 4 * 2 * wide * wide * rows, bytes_accessed=8 << 20, transcendentals=0
        ),
        name="sweep",
    )(centres, spot, extended, mine, other, measured, left_op, right_op)


def shifted(block, axis, distance):
    devices = range(lax.axis_size(axis))
    return lax.ppermute(block, axis, [(i - distance, i) for i in devices if i - distance in devices])


def extended_2(tile):
    side = tile.shape[1]
    above, below = shifted(tile, "gy", 1), shifted(tile, "gy", -1)
    tall = jnp.concatenate([above, tile, below], axis=1)
    before, after = shifted(tall, "gx", 1), shifted(tall, "gx", -1)
    blank = jnp.zeros((2, 3 * side, side), jnp.float32)
    return jnp.concatenate([before, tall, after, blank], axis=2)


def folded(top, middle, bottom):
    side = middle.shape[1]
    strip = middle + shifted(bottom, "gy", 1) + shifted(top, "gy", -1)
    before = shifted(strip[:, :, 2 * side : 3 * side], "gx", 1)
    after = shifted(strip[:, :, :side], "gx", -1)
    return strip[:, :, side : 2 * side] + before + after


def summed_over_z(block):
    for flip in Z_STEPS:
        block = block + exchange(block, flip)
    return block


def summed(keep, send):
    block = keep + exchange(send, CORE)
    for flips in PLANE_STEPS:
        half = block.shape[0] // 2
        block = block[:half] + exchange(block[half:], flips)
    return summed_over_z(block[0])


def gathered(block):
    block = block[None]
    for flips in reversed(PLANE_STEPS):
        block = jnp.concatenate([block, exchange(block, flips)], axis=0)
    return block, exchange(block, CORE)


def local(object_field, probe_modes, positions, amplitudes):
    side = amplitudes.shape[-1]
    centres = positions.reshape(-1, 2)
    measured = amplitudes.reshape(-1, side, side)
    left_op = table(side)
    left_op, right_op = jnp.asarray(left_op), jnp.asarray(left_op.T)
    gx, gy = lax.axis_index("gx"), lax.axis_index("gy")
    z = gy % 8
    spot = jnp.stack([gx % 2, gx // 4, (gy // 8) * 2 + (gx // 2) % 2]).astype(jnp.int32)

    own = probe_modes.reshape(1, 8, side)
    own = lax.dynamic_update_slice(jnp.zeros((8, 8, side), jnp.float32), own, (z, 0, 0))
    own = summed_over_z(own)
    current = object_field
    for iteration in range(ITERS):
        mine, other = gathered(own)
        extended = extended_2(current)
        keep, send, top, middle, bottom = sweep(
            centres, spot, extended, mine, other, measured, left_op, right_op
        )
        total = summed(keep, send)
        sums = folded(top, middle, bottom)
        current = current - sums[0:2] / (sums[2] + OBJECT_REG)
        weight = total[8].reshape(2, 1, 4, side)
        weight = jnp.broadcast_to(weight, (2, 2, 4, side)).reshape(1, 2, 8, side)
        change = total[:8].reshape(4, 2, 8, side) / (weight + PROBE_REG)
        own = own - change.reshape(8, 8, side)
    own = lax.dynamic_slice(own, (z, 0, 0), (1, 8, side))
    return (current, own.reshape(2, 4, side))


def solution(mesh):
    return jax.shard_map(
        local,
        mesh=mesh,
        in_specs=(
            P(None, "gy", "gx"),
            P(None, ("gy", "gx"), None),
            P("gy", "gx", None, None),
            P("gy", "gx", None, None, None),
        ),
        out_specs=(P(None, "gy", "gx"), P(None, ("gy", "gx"), None)),
        check_vma=False,
    )
```

time: 1360 us -> 232 us (0.17)
  waiting for transfers between devices: 861 us -> 94.6 us
  local copies, waits for them, and re-layouts: 158 us -> 3.13 us
  other arithmetic: 136 us -> 2.43 us
  loops' own time: 88.1 us -> 0 us
  matrix products: 46.9 us -> 0 us
  starting transfers between devices: 51.3 us -> 96.3 us
  Pallas kernels: 0 us -> 30.4 us
    psum x2 -> x0, waiting for transfers between devices: 482 us -> none  [local(): totals, weight_total = lax.psum((grad_rows, weight_probe), ('gy', 'gx'))]
    all_gather x1 -> x0, waiting for transfers between devices: 362 us -> none  [local(): gathered = lax.all_gather(probe_modes, ('gy', 'gx'), axis=1, tiled=True)]
    another operation x2 -> x0, loops' own time: 88.1 us -> none  [local(): lax.scan(visit, initial, (centres[:, 0], centres[:, 1], measured_all))]
    add x102 -> x22, other arithmetic: 86.7 us -> 0.62 us  [the longest x2 0.19 us: folded(): return strip[:, :, side:2 * side] + before + after]
    ppermute x16 -> x45, waiting for transfers between devices: 16.9 us -> 94.6 us  [the longest x29 82 us: exchange(): lax.ppermute(block, ('gx', 'gy'), [(mesh_place(a), mesh_place(b)) for a,...]
    dynamic_update_slice x24 -> x1, local copies, waits for them, and re-layouts: 66.4 us -> 0.01 us  [local(): lax.dynamic_update_slice(jnp.zeros((8, 8, side), jnp.float32), own, (z, 0...]
    while x336 -> x0, local copies, waits for them, and re-layouts: 49.5 us -> none
    dot_general x48 -> x0, matrix products: 46.9 us -> none  [transform(): jnp.einsum('crmq,cqdk->drmk', halfway, right_op, preferred_element_type=j...]
  transfers between devices with their start and end apart: 19 -> 45, of which waited for: 12 -> 29; matrix products, arithmetic and copies ran while one was open for 1% -> 1% of each run, Pallas kernels for 0% -> 0%
where the time goes in v1:
time: 232 us; the launch traced here: 228 us
  starting transfers between devices  96.3 us (42%)
  waiting for transfers between devices  94.6 us (41%)
  Pallas kernels  30.4 us (13%)
  local copies, waits for them, and re-layouts  3.13 us (1%)
  other arithmetic  2.43 us (1%)
    ppermute x29, waiting for transfers between devices, exchange(): lax.ppermute(block, ('gx', 'gy'), [(mesh_place(a), mesh_place(b)) for a,...  82 us
    ppermute x29, starting transfers between devices, exchange(): lax.ppermute(block, ('gx', 'gy'), [(mesh_place(a), mesh_place(b)) for a,...  48.9 us
    ppermute x16, starting transfers between devices, shifted(): lax.ppermute(block, axis, [(i - distance, i) for i in devices if i - dist...  47.4 us
    pallas_call x2, Pallas kernels, sweep(): pl.pallas_call(sweep_kernel, in_specs=[smem, smem] + [vmem] * 6, out_spec...  30.4 us
    ppermute x16, waiting for transfers between devices, shifted(): lax.ppermute(block, axis, [(i - distance, i) for i in devices if i - dist...  12.5 us
  transfers between devices with their start and end apart: 45, of which 29 were waited for; matrix products, arithmetic and copies ran while one was open for 1% of the time, Pallas kernels for 0%

profile of v1, /device:TPU:16, one launch (start us, length us, event | category | flops | bytes accessed | tf_op | source)
XLA Modules:
  0.0 228.3 jit_solution(13117393999180736301)
XLA Ops:
  10.4 6.0 %collective-permute-start.6 = (f32[8,8,128]{2,1,0:T(8,128)S(1)}, f32[8,8,128]{2,1,0:T(8,128)S(1)}, u32[]{:S(2)}, u32[]{:S(2)}) collective-permute-start(f32[8,8,128]{2,1,0:T(8,128)S(1)} %add.146), channel_id=1, source_target_pairs={{0,6},{16,22},{32,38},{48,54},{64,70},{80,86},{96,102},{112,118},{... | collective-permute-start | bytes 98312 | tf_op jit(solution)/shard_map/ppermute | solution.py:34
  29.5 5.8 %collective-permute-start.1 = (f32[2,64,64]{2,1,0:T(8,128)S(1)}, f32[2,64,64]{2,1,0:T(8,128)S(1)}, u32[]{:S(2)}, u32[]{:S(2)}) collective-permute-start(f32[2,64,64]{2,1,0:T(8,128)S(1)} %copy-done.3), channel_id=1, source_target_pairs={{1,0},{2,1},{3,2},{4,3},{5,4},{6,5},{7,6},{8,7},{9,8},{10,9},{11,1... | collective-permute-start | bytes 98312 | tf_op jit(solution)/shard_map/ppermute | solution.py:233
  36.4 6.3 %collective-permute-done.10 = f32[8,8,8,128]{3,2,1,0:T(8,128)S(1)} collective-permute-done((f32[8,8,8,128]{3,2,1,0:T(8,128)S(1)}, f32[8,8,8,128]{3,2,1,0:T(8,128)S(1)}, u32[]{:S(2)}, u32[]{:S(2)}) %collective-permute-start.10) | collective-permute-done | bytes 262176 | tf_op jit(solution)/shard_map/ppermute | solution.py:34
  48.5 15.2 %sweep.2 = (f32[16,9,8,128]{3,2,1,0:T(8,128)S(1)}, f32[16,9,8,128]{3,2,1,0:T(8,128)S(1)}, f32[3,64,256]{2,1,0:T(8,128)S(1)}, f32[3,64,256]{2,1,0:T(8,128)S(1)}, f32[3,64,256]{2,1,0:T(8,128)S(1)}) custom-call(s32[12,2]{1,0:T(8,128)S(1)} %copy.8.pos_ref, s32[3]{0:T(128)S(1)} %pad_add_fusion.spot_ref, f32[2,192,256]{2,1,0:T(8,128)S(1)} %maximum_maximum_fusion.ext_ref, ...), custom_call_target="tpu_custom_call" | custom-call | flops 6442450944 | bytes 8388608 | tf_op jit(solution)/shard_map/sweep/pallas_call | solution.py:207
  63.7 6.1 %collective-permute-start.20 = (f32[16,9,8,128]{3,2,1,0:T(8,128)S(1)}, f32[16,9,8,128]{3,2,1,0:T(8,128)S(1)}, u32[]{:S(2)}, u32[]{:S(2)}) collective-permute-start(f32[16,9,8,128]{3,2,1,0:T(8,128)S(1)} %get-tuple-element.16), channel_id=1, source_target_pairs={{0,16},{16,0},{32,48},{48,32},{64,80},{80,64},{96,112},{112,96},{1... | collective-permute-start | bytes 1769480 | tf_op jit(solution)/shard_map/ppermute | solution.py:34
  72.1 6.3 %collective-permute-done.21 = f32[8,9,8,128]{3,2,1,0:T(8,128)S(1)} collective-permute-done((f32[8,9,8,128]{3,2,1,0:T(8,128)S(1)}, f32[8,9,8,128]{3,2,1,0:T(8,128)S(1)}, u32[]{:S(2)}, u32[]{:S(2)}) %collective-permute-start.21) | collective-permute-done | bytes 294944 | tf_op jit(solution)/shard_map/ppermute | solution.py:34
  78.5 4.0 %collective-permute-start.22 = (f32[4,9,8,128]{3,2,1,0:T(8,128)S(1)}, f32[4,9,8,128]{3,2,1,0:T(8,128)S(1)}, u32[]{:S(2)}, u32[]{:S(2)}) collective-permute-start(f32[4,9,8,128]{3,2,1,0:T(8,128)S(1)} %slice.128), channel_id=1, source_target_pairs={{0,32},{16,80},{32,0},{48,112},{64,96},{80,16},{96,64},{112,48},{1... | collective-permute-start | bytes 442376 | tf_op jit(solution)/shard_map/ppermute | solution.py:34
  86.6 4.7 %collective-permute-done.23 = f32[2,9,8,128]{3,2,1,0:T(8,128)S(1)} collective-permute-done((f32[2,9,8,128]{3,2,1,0:T(8,128)S(1)}, f32[2,9,8,128]{3,2,1,0:T(8,128)S(1)}, u32[]{:S(2)}, u32[]{:S(2)}) %collective-permute-start.23) | collective-permute-done | bytes 73760 | tf_op jit(solution)/shard_map/ppermute | solution.py:34
  93.6 7.5 %collective-permute-start.13 = (f32[3,64,256]{2,1,0:T(8,128)S(1)}, f32[3,64,256]{2,1,0:T(8,128)S(1)}, u32[]{:S(2)}, u32[]{:S(2)}) collective-permute-start(f32[3,64,256]{2,1,0:T(8,128)S(1)} %get-tuple-element.14), channel_id=1, source_target_pairs={{1,0},{2,1},{3,2},{4,3},{5,4},{6,5},{7,6},{8,7},{9,8},{10,9},{11,1... | collective-permute-start | bytes 589832 | tf_op jit(solution)/shard_map/ppermute | solution.py:233
  101.3 3.9 %collective-permute-done.25 = f32[9,8,128]{2,1,0:T(8,128)S(1)} collective-permute-done((f32[9,8,128]{2,1,0:T(8,128)S(1)}, f32[9,8,128]{2,1,0:T(8,128)S(1)}, u32[]{:S(2)}, u32[]{:S(2)}) %collective-permute-start.25) | collective-permute-done | bytes 36896 | tf_op jit(solution)/shard_map/ppermute | solution.py:34
  105.3 4.8 %collective-permute-done.26 = f32[9,8,128]{2,1,0:T(8,128)S(1)} collective-permute-done((f32[9,8,128]{2,1,0:T(8,128)S(1)}, f32[9,8,128]{2,1,0:T(8,128)S(1)}, u32[]{:S(2)}, u32[]{:S(2)}) %collective-permute-start.26) | collective-permute-done | bytes 36896 | tf_op jit(solution)/shard_map/ppermute | solution.py:34
  110.2 6.0 %collective-permute-done.27 = f32[9,8,128]{2,1,0:T(8,128)S(1)} collective-permute-done((f32[9,8,128]{2,1,0:T(8,128)S(1)}, f32[9,8,128]{2,1,0:T(8,128)S(1)}, u32[]{:S(2)}, u32[]{:S(2)}) %collective-permute-start.27) | collective-permute-done | bytes 36896 | tf_op jit(solution)/shard_map/ppermute | solution.py:34
  121.0 4.7 %collective-permute-start.29 = (f32[2,8,8,128]{3,2,1,0:T(8,128)S(1)}, f32[2,8,8,128]{3,2,1,0:T(8,128)S(1)}, u32[]{:S(2)}, u32[]{:S(2)}) collective-permute-start(f32[2,8,8,128]{3,2,1,0:T(8,128)S(1)} %pad_maximum_fusion.6), channel_id=1, source_target_pairs={{0,192},{16,56},{32,224},{48,24},{64,128},{80,120},{96,160},{112,8... | collective-permute-start | bytes 196616 | tf_op jit(solution)/shard_map/ppermute | solution.py:34
  127.9 3.5 %collective-permute-start.30 = (f32[4,8,8,128]{3,2,1,0:T(8,128)S(1)}, f32[4,8,8,128]{3,2,1,0:T(8,128)S(1)}, u32[]{:S(2)}, u32[]{:S(2)}) collective-permute-start(f32[4,8,8,128]{3,2,1,0:T(8,128)S(1)} %pad_maximum_fusion.4), channel_id=1, source_target_pairs={{0,32},{16,80},{32,0},{48,112},{64,96},{80,16},{96,64},{112,48},{1... | collective-permute-start | bytes 393224 | tf_op jit(solution)/shard_map/ppermute | solution.py:34
  134.5 6.3 %collective-permute-done.31 = f32[8,8,8,128]{3,2,1,0:T(8,128)S(1)} collective-permute-done((f32[8,8,8,128]{3,2,1,0:T(8,128)S(1)}, f32[8,8,8,128]{3,2,1,0:T(8,128)S(1)}, u32[]{:S(2)}, u32[]{:S(2)}) %collective-permute-start.31) | collective-permute-done | bytes 262176 | tf_op jit(solution)/shard_map/ppermute | solution.py:34
  143.4 3.3 %collective-permute-start.16 = (f32[2,64,64]{2,1,0:T(8,128)S(1)}, f32[2,64,64]{2,1,0:T(8,128)S(1)}, u32[]{:S(2)}, u32[]{:S(2)}) collective-permute-start(f32[2,64,64]{2,1,0:T(8,128)S(1)} %fusion.3), channel_id=1, source_target_pairs={{0,1},{1,2},{2,3},{3,4},{4,5},{5,6},{6,7},{7,8},{8,9},{9,10},{10,1... | collective-permute-start | bytes 98312 | tf_op jit(solution)/shard_map/ppermute | solution.py:233
  147.3 5.9 %collective-permute-done.16 = f32[2,64,64]{2,1,0:T(8,128)S(1)} collective-permute-done((f32[2,64,64]{2,1,0:T(8,128)S(1)}, f32[2,64,64]{2,1,0:T(8,128)S(1)}, u32[]{:S(2)}, u32[]{:S(2)}) %collective-permute-start.16) | collective-permute-done | bytes 32800 | tf_op jit(solution)/shard_map/ppermute | solution.py:233
  158.8 15.2 %sweep.3 = (f32[16,9,8,128]{3,2,1,0:T(8,128)S(1)}, f32[16,9,8,128]{3,2,1,0:T(8,128)S(1)}, f32[3,64,256]{2,1,0:T(8,128)S(1)}, f32[3,64,256]{2,1,0:T(8,128)S(1)}, f32[3,64,256]{2,1,0:T(8,128)S(1)}) custom-call(s32[12,2]{1,0:T(8,128)S(1)} %copy.8.pos_ref, s32[3]{0:T(128)S(1)} %pad_add_fusion.spot_ref, f32[2,192,256]{2,1,0:T(8,128)S(1)} %maximum_maximum_fusion.1.ext_ref, ...), custom_call_target="tpu_custom_call" | custom-call | flops 6442450944 | bytes 8388608 | tf_op jit(solution)/shard_map/sweep/pallas_call | solution.py:207
  174.0 5.0 %collective-permute-start.37 = (f32[16,9,8,128]{3,2,1,0:T(8,128)S(1)}, f32[16,9,8,128]{3,2,1,0:T(8,128)S(1)}, u32[]{:S(2)}, u32[]{:S(2)}) collective-permute-start(f32[16,9,8,128]{3,2,1,0:T(8,128)S(1)} %get-tuple-element.21), channel_id=1, source_target_pairs={{0,16},{16,0},{32,48},{48,32},{64,80},{80,64},{96,112},{112,96},{1... | collective-permute-start | bytes 1769480 | tf_op jit(solution)/shard_map/ppermute | solution.py:34
  180.9 6.7 %collective-permute-done.38 = f32[8,9,8,128]{3,2,1,0:T(8,128)S(1)} collective-permute-done((f32[8,9,8,128]{3,2,1,0:T(8,128)S(1)}, f32[8,9,8,128]{3,2,1,0:T(8,128)S(1)}, u32[]{:S(2)}, u32[]{:S(2)}) %collective-permute-start.38) | collective-permute-done | bytes 294944 | tf_op jit(solution)/shard_map/ppermute | solution.py:34
  187.7 4.1 %collective-permute-start.39 = (f32[4,9,8,128]{3,2,1,0:T(8,128)S(1)}, f32[4,9,8,128]{3,2,1,0:T(8,128)S(1)}, u32[]{:S(2)}, u32[]{:S(2)}) collective-permute-start(f32[4,9,8,128]{3,2,1,0:T(8,128)S(1)} %slice.143), channel_id=1, source_target_pairs={{0,32},{16,80},{32,0},{48,112},{64,96},{80,16},{96,64},{112,48},{1... | collective-permute-start | bytes 442376 | tf_op jit(solution)/shard_map/ppermute | solution.py:34
  193.6 7.5 %collective-permute-start.34 = (f32[3,64,256]{2,1,0:T(8,128)S(1)}, f32[3,64,256]{2,1,0:T(8,128)S(1)}, u32[]{:S(2)}, u32[]{:S(2)}) collective-permute-start(f32[3,64,256]{2,1,0:T(8,128)S(1)} %get-tuple-element.19), channel_id=1, source_target_pairs={{1,0},{2,1},{3,2},{4,3},{5,4},{6,5},{7,6},{8,7},{9,8},{10,9},{11,1... | collective-permute-start | bytes 589832 | tf_op jit(solution)/shard_map/ppermute | solution.py:233
  215.0 5.3 %collective-permute-done.43 = f32[9,8,128]{2,1,0:T(8,128)S(1)} collective-permute-done((f32[9,8,128]{2,1,0:T(8,128)S(1)}, f32[9,8,128]{2,1,0:T(8,128)S(1)}, u32[]{:S(2)}, u32[]{:S(2)}) %collective-permute-start.43) | collective-permute-done | bytes 36896 | tf_op jit(solution)/shard_map/ppermute | solution.py:34
  220.9 5.4 %collective-permute-done.44 = f32[9,8,128]{2,1,0:T(8,128)S(1)} collective-permute-done((f32[9,8,128]{2,1,0:T(8,128)S(1)}, f32[9,8,128]{2,1,0:T(8,128)S(1)}, u32[]{:S(2)}, u32[]{:S(2)}) %collective-permute-start.44) | collective-permute-done | bytes 36896 | tf_op jit(solution)/shard_map/ppermute | solution.py:34
  (154 shorter events, 77.3 us)
Async XLA Ops:
  10.4 7.9 %collective-permute-start.6 = (f32[8,8,128]{2,1,0:T(8,128)S(1)}, f32[8,8,128]{2,1,0:T(8,128)S(1)}, u32[]{:S(2)}, u32[]{:S(2)}) collective-permute-start(f32[8,8,128]{2,1,0:T(8,128)S(1)} %add.146), channel_id=1, source_target_pairs={{0,6},{16,22},{32,38},{48,54},{64,70},{80,86},{96,102},{112,118},{... | collective-permute-start | bytes 98312 | tf_op jit(solution)/shard_map/ppermute | solution.py:34
  25.1 11.2 %collective-permute-start = (f32[2,64,64]{2,1,0:T(8,128)S(1)}, f32[2,64,64]{2,1,0:T(8,128)S(1)}, u32[]{:S(2)}, u32[]{:S(2)}) collective-permute-start(f32[2,64,64]{2,1,0:T(8,128)S(1)} %copy-done.3), channel_id=1, source_target_pairs={{0,1},{1,2},{2,3},{3,4},{4,5},{5,6},{6,7},{7,8},{8,9},{9,10},{10,1... | collective-permute-start | bytes 98312 | tf_op jit(solution)/shard_map/ppermute | solution.py:233
  28.1 8.1 %collective-permute-start.9 = (f32[4,8,8,128]{3,2,1,0:T(8,128)S(1)}, f32[4,8,8,128]{3,2,1,0:T(8,128)S(1)}, u32[]{:S(2)}, u32[]{:S(2)}) collective-permute-start(f32[4,8,8,128]{3,2,1,0:T(8,128)S(1)} %pad_maximum_fusion.3), channel_id=1, source_target_pairs={{0,32},{16,80},{32,0},{48,112},{64,96},{80,16},{96,64},{112,48},{1... | collective-permute-start | bytes 393224 | tf_op jit(solution)/shard_map/ppermute | solution.py:34
  29.5 13.4 %collective-permute-start.1 = (f32[2,64,64]{2,1,0:T(8,128)S(1)}, f32[2,64,64]{2,1,0:T(8,128)S(1)}, u32[]{:S(2)}, u32[]{:S(2)}) collective-permute-start(f32[2,64,64]{2,1,0:T(8,128)S(1)} %copy-done.3), channel_id=1, source_target_pairs={{1,0},{2,1},{3,2},{4,3},{5,4},{6,5},{7,6},{8,7},{9,8},{10,9},{11,1... | collective-permute-start | bytes 98312 | tf_op jit(solution)/shard_map/ppermute | solution.py:233
  36.3 6.5 %collective-permute-start.10 = (f32[8,8,8,128]{3,2,1,0:T(8,128)S(1)}, f32[8,8,8,128]{3,2,1,0:T(8,128)S(1)}, u32[]{:S(2)}, u32[]{:S(2)}) collective-permute-start(f32[8,8,8,128]{3,2,1,0:T(8,128)S(1)} %pad_maximum_fusion), channel_id=1, source_target_pairs={{0,40},{16,208},{32,8},{48,240},{64,104},{80,144},{96,72},{112,176... | collective-permute-start | bytes 786440 | tf_op jit(solution)/shard_map/ppermute | solution.py:34
  63.7 7.8 %collective-permute-start.20 = (f32[16,9,8,128]{3,2,1,0:T(8,128)S(1)}, f32[16,9,8,128]{3,2,1,0:T(8,128)S(1)}, u32[]{:S(2)}, u32[]{:S(2)}) collective-permute-start(f32[16,9,8,128]{3,2,1,0:T(8,128)S(1)} %get-tuple-element.16), channel_id=1, source_target_pairs={{0,16},{16,0},{32,48},{48,32},{64,80},{80,64},{96,112},{112,96},{1... | collective-permute-start | bytes 1769480 | tf_op jit(solution)/shard_map/ppermute | solution.py:34
  71.6 6.8 %collective-permute-start.21 = (f32[8,9,8,128]{3,2,1,0:T(8,128)S(1)}, f32[8,9,8,128]{3,2,1,0:T(8,128)S(1)}, u32[]{:S(2)}, u32[]{:S(2)}) collective-permute-start(f32[8,9,8,128]{3,2,1,0:T(8,128)S(1)} %slice.126), channel_id=1, source_target_pairs={{0,40},{16,208},{32,8},{48,240},{64,104},{80,144},{96,72},{112,176... | collective-permute-start | bytes 884744 | tf_op jit(solution)/shard_map/ppermute | solution.py:34
  78.5 7.1 %collective-permute-start.22 = (f32[4,9,8,128]{3,2,1,0:T(8,128)S(1)}, f32[4,9,8,128]{3,2,1,0:T(8,128)S(1)}, u32[]{:S(2)}, u32[]{:S(2)}) collective-permute-start(f32[4,9,8,128]{3,2,1,0:T(8,128)S(1)} %slice.128), channel_id=1, source_target_pairs={{0,32},{16,80},{32,0},{48,112},{64,96},{80,16},{96,64},{112,48},{1... | collective-permute-start | bytes 442376 | tf_op jit(solution)/shard_map/ppermute | solution.py:34
  91.3 9.9 %collective-permute-start.24 = (f32[1,9,8,128]{3,2,1,0:T(8,128)S(1)}, f32[1,9,8,128]{3,2,1,0:T(8,128)S(1)}, u32[]{:S(2)}, u32[]{:S(2)}) collective-permute-start(f32[1,9,8,128]{3,2,1,0:T(8,128)S(1)} %slice.132), channel_id=1, source_target_pairs={{0,64},{16,48},{32,96},{48,16},{64,0},{80,112},{96,32},{112,80},{1... | collective-permute-start | bytes 110600 | tf_op jit(solution)/shard_map/ppermute | solution.py:34
  91.7 18.4 %collective-permute-start.12 = (f32[3,64,256]{2,1,0:T(8,128)S(1)}, f32[3,64,256]{2,1,0:T(8,128)S(1)}, u32[]{:S(2)}, u32[]{:S(2)}) collective-permute-start(f32[3,64,256]{2,1,0:T(8,128)S(1)} %get-tuple-element.13), channel_id=1, source_target_pairs={{0,1},{1,2},{2,3},{3,4},{4,5},{5,6},{6,7},{7,8},{8,9},{9,10},{10,1... | collective-permute-start | bytes 589832 | tf_op jit(solution)/shard_map/ppermute | solution.py:233
  93.6 16.5 %collective-permute-start.13 = (f32[3,64,256]{2,1,0:T(8,128)S(1)}, f32[3,64,256]{2,1,0:T(8,128)S(1)}, u32[]{:S(2)}, u32[]{:S(2)}) collective-permute-start(f32[3,64,256]{2,1,0:T(8,128)S(1)} %get-tuple-element.14), channel_id=1, source_target_pairs={{1,0},{2,1},{3,2},{4,3},{5,4},{6,5},{7,6},{8,7},{9,8},{10,9},{11,1... | collective-permute-start | bytes 589832 | tf_op jit(solution)/shard_map/ppermute | solution.py:233
  118.3 7.3 %collective-permute-start.14 = (f32[3,64,64]{2,1,0:T(8,128)S(1)}, f32[3,64,64]{2,1,0:T(8,128)S(1)}, u32[]{:S(2)}, u32[]{:S(2)}) collective-permute-start(f32[3,64,64]{2,1,0:T(8,128)S(1)} %get-tuple-element.26), channel_id=1, source_target_pairs={{0,16},{16,32},{32,48},{48,64},{64,80},{80,96},{96,112},{112,128},... | collective-permute-start | bytes 147464 | tf_op jit(solution)/shard_map/ppermute | solution.py:233
  121.0 6.9 %collective-permute-start.29 = (f32[2,8,8,128]{3,2,1,0:T(8,128)S(1)}, f32[2,8,8,128]{3,2,1,0:T(8,128)S(1)}, u32[]{:S(2)}, u32[]{:S(2)}) collective-permute-start(f32[2,8,8,128]{3,2,1,0:T(8,128)S(1)} %pad_maximum_fusion.6), channel_id=1, source_target_pairs={{0,192},{16,56},{32,224},{48,24},{64,128},{80,120},{96,160},{112,8... | collective-permute-start | bytes 196616 | tf_op jit(solution)/shard_map/ppermute | solution.py:34
  127.9 6.4 %collective-permute-start.30 = (f32[4,8,8,128]{3,2,1,0:T(8,128)S(1)}, f32[4,8,8,128]{3,2,1,0:T(8,128)S(1)}, u32[]{:S(2)}, u32[]{:S(2)}) collective-permute-start(f32[4,8,8,128]{3,2,1,0:T(8,128)S(1)} %pad_maximum_fusion.4), channel_id=1, source_target_pairs={{0,32},{16,80},{32,0},{48,112},{64,96},{80,16},{96,64},{112,48},{1... | collective-permute-start | bytes 393224 | tf_op jit(solution)/shard_map/ppermute | solution.py:34
  134.3 6.5 %collective-permute-start.31 = (f32[8,8,8,128]{3,2,1,0:T(8,128)S(1)}, f32[8,8,8,128]{3,2,1,0:T(8,128)S(1)}, u32[]{:S(2)}, u32[]{:S(2)}) collective-permute-start(f32[8,8,8,128]{3,2,1,0:T(8,128)S(1)} %pad_maximum_fusion.1), channel_id=1, source_target_pairs={{0,40},{16,208},{32,8},{48,240},{64,104},{80,144},{96,72},{112,176... | collective-permute-start | bytes 786440 | tf_op jit(solution)/shard_map/ppermute | solution.py:34
  140.8 18.0 %collective-permute-start.32 = (f32[16,8,8,128]{3,2,1,0:T(8,128)S(1)}, f32[16,8,8,128]{3,2,1,0:T(8,128)S(1)}, u32[]{:S(2)}, u32[]{:S(2)}) collective-permute-start(f32[16,8,8,128]{3,2,1,0:T(8,128)S(1)} %constant_dynamic-update-slice_fusion.8.mine_ref), channel_id=1, source_target_pairs={{0,16},{16,0},{32,48},{48,32},{64,80},{80,64},{96,112},{112,96},{1... | collective-permute-start | bytes 1572872 | tf_op jit(solution)/shard_map/ppermute | solution.py:34
  140.9 6.4 %collective-permute-start.17 = (f32[2,64,64]{2,1,0:T(8,128)S(1)}, f32[2,64,64]{2,1,0:T(8,128)S(1)}, u32[]{:S(2)}, u32[]{:S(2)}) collective-permute-start(f32[2,64,64]{2,1,0:T(8,128)S(1)} %fusion.3), channel_id=1, source_target_pairs={{1,0},{2,1},{3,2},{4,3},{5,4},{6,5},{7,6},{8,7},{9,8},{10,9},{11,1... | collective-permute-start | bytes 98312 | tf_op jit(solution)/shard_map/ppermute | solution.py:233
  143.4 9.8 %collective-permute-start.16 = (f32[2,64,64]{2,1,0:T(8,128)S(1)}, f32[2,64,64]{2,1,0:T(8,128)S(1)}, u32[]{:S(2)}, u32[]{:S(2)}) collective-permute-start(f32[2,64,64]{2,1,0:T(8,128)S(1)} %fusion.3), channel_id=1, source_target_pairs={{0,1},{1,2},{2,3},{3,4},{4,5},{5,6},{6,7},{7,8},{8,9},{9,10},{10,1... | collective-permute-start | bytes 98312 | tf_op jit(solution)/shard_map/ppermute | solution.py:233
  174.0 6.7 %collective-permute-start.37 = (f32[16,9,8,128]{3,2,1,0:T(8,128)S(1)}, f32[16,9,8,128]{3,2,1,0:T(8,128)S(1)}, u32[]{:S(2)}, u32[]{:S(2)}) collective-permute-start(f32[16,9,8,128]{3,2,1,0:T(8,128)S(1)} %get-tuple-element.21), channel_id=1, source_target_pairs={{0,16},{16,0},{32,48},{48,32},{64,80},{80,64},{96,112},{112,96},{1... | collective-permute-start | bytes 1769480 | tf_op jit(solution)/shard_map/ppermute | solution.py:34
  180.8 6.8 %collective-permute-start.38 = (f32[8,9,8,128]{3,2,1,0:T(8,128)S(1)}, f32[8,9,8,128]{3,2,1,0:T(8,128)S(1)}, u32[]{:S(2)}, u32[]{:S(2)}) collective-permute-start(f32[8,9,8,128]{3,2,1,0:T(8,128)S(1)} %slice.141), channel_id=1, source_target_pairs={{0,40},{16,208},{32,8},{48,240},{64,104},{80,144},{96,72},{112,176... | collective-permute-start | bytes 884744 | tf_op jit(solution)/shard_map/ppermute | solution.py:34
  187.7 13.5 %collective-permute-start.39 = (f32[4,9,8,128]{3,2,1,0:T(8,128)S(1)}, f32[4,9,8,128]{3,2,1,0:T(8,128)S(1)}, u32[]{:S(2)}, u32[]{:S(2)}) collective-permute-start(f32[4,9,8,128]{3,2,1,0:T(8,128)S(1)} %slice.143), channel_id=1, source_target_pairs={{0,32},{16,80},{32,0},{48,112},{64,96},{80,16},{96,64},{112,48},{1... | collective-permute-start | bytes 442376 | tf_op jit(solution)/shard_map/ppermute | solution.py:34
  191.7 11.3 %collective-permute-start.33 = (f32[3,64,256]{2,1,0:T(8,128)S(1)}, f32[3,64,256]{2,1,0:T(8,128)S(1)}, u32[]{:S(2)}, u32[]{:S(2)}) collective-permute-start(f32[3,64,256]{2,1,0:T(8,128)S(1)} %get-tuple-element.18), channel_id=1, source_target_pairs={{0,1},{1,2},{2,3},{3,4},{4,5},{5,6},{6,7},{7,8},{8,9},{9,10},{10,1... | collective-permute-start | bytes 589832 | tf_op jit(solution)/shard_map/ppermute | solution.py:233
  193.6 10.7 %collective-permute-start.34 = (f32[3,64,256]{2,1,0:T(8,128)S(1)}, f32[3,64,256]{2,1,0:T(8,128)S(1)}, u32[]{:S(2)}, u32[]{:S(2)}) collective-permute-start(f32[3,64,256]{2,1,0:T(8,128)S(1)} %get-tuple-element.19), channel_id=1, source_target_pairs={{1,0},{2,1},{3,2},{4,3},{5,4},{6,5},{7,6},{8,7},{9,8},{10,9},{11,1... | collective-permute-start | bytes 589832 | tf_op jit(solution)/shard_map/ppermute | solution.py:233
  220.2 6.1 %collective-permute-start.44 = (f32[9,8,128]{2,1,0:T(8,128)S(1)}, f32[9,8,128]{2,1,0:T(8,128)S(1)}, u32[]{:S(2)}, u32[]{:S(2)}) collective-permute-start(f32[9,8,128]{2,1,0:T(8,128)S(1)} %add.175), channel_id=1, source_target_pairs={{0,6},{16,22},{32,38},{48,54},{64,70},{80,86},{96,102},{112,118},{... | collective-permute-start | bytes 110600 | tf_op jit(solution)/shard_map/ppermute | solution.py:34
  (29 other events, 123.4 us)

commit v2 on v1

--- a/solution.py
+++ b/solution.py
@@ -16,10 +16,8 @@
 
 BAND = 32
 DEVICES = 256
-CORE = 1
 Y_FAR, Y_NEAR = 0b10000010, 0b00000010
 X_FAR, X_NEAR = 0b00001100, 0b00000100
-Z_STEPS = (0b00010000, 0b00100000, 0b01100000)
 PLANE_STEPS = ((Y_FAR, X_FAR), (Y_NEAR, X_NEAR), (X_FAR, Y_FAR), (X_NEAR, Y_NEAR))
 
 
@@ -27,11 +25,29 @@
     return (device % 16) * 16 + device // 16
 
 
-def exchange(block, flips):
-    if isinstance(flips, int):
-        flips = (flips, flips)
-    pairs = [(d, d ^ flips[d & 1]) for d in range(DEVICES)]
-    return lax.ppermute(block, ("gx", "gy"), [(mesh_place(a), mesh_place(b)) for a, b in pairs])
+def exchange(block, partner):
+    pairs = [(mesh_place(d), mesh_place(partner(d))) for d in range(DEVICES)]
+    return lax.ppermute(block, ("gx", "gy"), pairs)
+
+
+def other_core(block):
+    return exchange(block, lambda d: d ^ 1)
+
+
+def plane_partner(block, step):
+    return exchange(block, lambda d: d ^ PLANE_STEPS[step][d & 1])
+
+
+def z_even_pair(block):
+    return exchange(block, lambda d: d ^ 16)
+
+
+def z_odd_pair(block):
+    def partner(d):
+        z = d >> 4 & 7
+        return d & ~112 | (z + (1 if z % 2 else -1)) % 8 << 4
+
+    return exchange(block, partner)
 
 
 def table(side):
@@ -233,42 +249,38 @@
     return lax.ppermute(block, axis, [(i - distance, i) for i in devices if i - distance in devices])
 
 
-def extended_2(tile):
-    side = tile.shape[1]
-    above, below = shifted(tile, "gy", 1), shifted(tile, "gy", -1)
-    tall = jnp.concatenate([above, tile, below], axis=1)
+def tall_of(tile):
+    return jnp.concatenate([shifted(tile, "gy", 1), tile, shifted(tile, "gy", -1)], axis=1)
+
+
+def wide_of(tall):
+    side = tall.shape[2]
     before, after = shifted(tall, "gx", 1), shifted(tall, "gx", -1)
     blank = jnp.zeros((2, 3 * side, side), jnp.float32)
     return jnp.concatenate([before, tall, after, blank], axis=2)
 
 
-def folded(top, middle, bottom):
-    side = middle.shape[1]
-    strip = middle + shifted(bottom, "gy", 1) + shifted(top, "gy", -1)
+def folded_rows(top, middle, bottom):
+    return middle + shifted(bottom, "gy", 1) + shifted(top, "gy", -1)
+
+
+def folded_cols(strip):
+    side = strip.shape[1]
     before = shifted(strip[:, :, 2 * side : 3 * side], "gx", 1)
     after = shifted(strip[:, :, :side], "gx", -1)
     return strip[:, :, side : 2 * side] + before + after
 
 
-def summed_over_z(block):
-    for flip in Z_STEPS:
-        block = block + exchange(block, flip)
-    return block
-
-
-def summed(keep, send):
-    block = keep + exchange(send, CORE)
-    for flips in PLANE_STEPS:
-        half = block.shape[0] // 2
-        block = block[:half] + exchange(block[half:], flips)
-    return summed_over_z(block[0])
-
-
-def gathered(block):
-    block = block[None]
-    for flips in reversed(PLANE_STEPS):
-        block = jnp.concatenate([block, exchange(block, flips)], axis=0)
-    return block, exchange(block, CORE)
+def halved(block, step):
+    half = block.shape[0] // 2
+    return block[:half] + plane_partner(block[half:], step)
+
+
+def doubled(block, step):
+    return jnp.concatenate([block, plane_partner(block, step)], axis=0)
+
+
+together = lax.optimization_barrier
 
 
 def local(object_field, probe_modes, positions, amplitudes):
@@ -278,28 +290,64 @@
     left_op = table(side)
     left_op, right_op = jnp.asarray(left_op), jnp.asarray(left_op.T)
     gx, gy = lax.axis_index("gx"), lax.axis_index("gy")
-    z = gy % 8
-    spot = jnp.stack([gx % 2, gx // 4, (gy // 8) * 2 + (gx // 2) % 2]).astype(jnp.int32)
-
-    own = probe_modes.reshape(1, 8, side)
-    own = lax.dynamic_update_slice(jnp.zeros((8, 8, side), jnp.float32), own, (z, 0, 0))
-    own = summed_over_z(own)
+    z = lax.bitwise_and(gy, 7)
+    y = lax.bitwise_and(lax.shift_right_logical(gy, 2), 2) + lax.bitwise_and(lax.shift_right_logical(gx, 1), 1)
+    spot = jnp.stack([lax.bitwise_and(gx, 1), lax.shift_right_logical(gx, 2), y]).astype(jnp.int32)
+    is_own = (jnp.arange(8) == z)[:, None, None]
+
     current = object_field
+    own = jnp.where(is_own, probe_modes.reshape(1, 8, side), 0.0)
+    first = own + z_even_pair(own)
+    second = z_odd_pair(first)
+    tall = tall_of(current)
+    third = z_even_pair(second)
+    third, tall = together((third, tall))
+    fourth = z_odd_pair(third)
+    own = (first + second) + (third + fourth)
+    extended = wide_of(tall)
+    mine = doubled(own[None], 3)
+    mine = doubled(mine, 2)
+    mine, extended = together((mine, extended))
+    mine = doubled(doubled(mine, 1), 0)
+
     for iteration in range(ITERS):
-        mine, other = gathered(own)
-        extended = extended_2(current)
+        other = other_core(mine)
         keep, send, top, middle, bottom = sweep(
             centres, spot, extended, mine, other, measured, left_op, right_op
         )
-        total = summed(keep, send)
-        sums = folded(top, middle, bottom)
+        block = keep + other_core(send)
+        block, top, middle, bottom = together((block, top, middle, bottom))
+        block = halved(block, 0)
+        strip = folded_rows(top, middle, bottom)
+        block = halved(block, 1)
+        block, strip = together((block, strip))
+        block = halved(block, 2)
+        sums = folded_cols(strip)
+        block = halved(block, 3)[0]
+        block, sums = together((block, sums))
+        first = block + z_even_pair(block)
         current = current - sums[0:2] / (sums[2] + OBJECT_REG)
+        if iteration < ITERS - 1:
+            tall = tall_of(current)
+        second = z_odd_pair(first)
+        if iteration < ITERS - 1:
+            second, tall = together((second, tall))
+            extended = wide_of(tall)
+        third = z_even_pair(second)
+        if iteration < ITERS - 1:
+            third, extended = together((third, extended))
+        fourth = z_odd_pair(third)
+        total = (first + second) + (third + fourth)
         weight = total[8].reshape(2, 1, 4, side)
         weight = jnp.broadcast_to(weight, (2, 2, 4, side)).reshape(1, 2, 8, side)
         change = total[:8].reshape(4, 2, 8, side) / (weight + PROBE_REG)
         own = own - change.reshape(8, 8, side)
-    own = lax.dynamic_slice(own, (z, 0, 0), (1, 8, side))
-    return (current, own.reshape(2, 4, side))
+        if iteration < ITERS - 1:
+            mine = own[None]
+            for step in (3, 2, 1, 0):
+                mine = doubled(mine, step)
+    probe_rows = jnp.sum(jnp.where(is_own, own, 0.0), axis=0)
+    return (current, probe_rows.reshape(2, 4, side))
 
 
 def solution(mesh):

time: 232 us -> 223 us (0.961)
  waiting for transfers between devices: 94.6 us -> 89.3 us
  starting transfers between devices: 96.3 us -> 92.9 us
    ppermute x29 -> x32, waiting for transfers between devices: 82 us -> 69.1 us  [exchange(): return lax.ppermute(block, ('gx', 'gy'), pairs)]
    ppermute x16, waiting for transfers between devices: 12.5 us -> 20.1 us  [shifted(): lax.ppermute(block, axis, [(i - distance, i) for i in devices if i - dist...]
    ppermute x29 -> x32, starting transfers between devices: 48.9 us -> 45.4 us  [exchange(): return lax.ppermute(block, ('gx', 'gy'), pairs)]
  transfers between devices with their start and end apart: 45 -> 48, of which waited for: 29 -> 35; matrix products, arithmetic and copies ran while one was open for 1% -> 1% of each run, Pallas kernels for 0% -> 0%
where the time goes in v2:
time: 223 us; the launch traced here: 220 us
  starting transfers between devices  92.9 us (42%)
  waiting for transfers between devices  89.3 us (40%)
  Pallas kernels  31 us (14%)
  other arithmetic  4.14 us (2%)
    ppermute x32, waiting for transfers between devices, exchange(): return lax.ppermute(block, ('gx', 'gy'), pairs)  69.1 us
    ppermute x16, starting transfers between devices, shifted(): lax.ppermute(block, axis, [(i - distance, i) for i in devices if i - dist...  47.5 us
    ppermute x32, starting transfers between devices, exchange(): return lax.ppermute(block, ('gx', 'gy'), pairs)  45.4 us
    pallas_call x2, Pallas kernels, sweep(): pl.pallas_call(sweep_kernel, in_specs=[smem, smem] + [vmem] * 6, out_spec...  31 us
    ppermute x16, waiting for transfers between devices, shifted(): lax.ppermute(block, axis, [(i - distance, i) for i in devices if i - dist...  20.1 us
  transfers between devices with their start and end apart: 48, of which 35 were waited for; matrix products, arithmetic and copies ran while one was open for 1% of the time, Pallas kernels for 0%

profile of v2, /device:TPU:16, one launch (start us, length us, event | category | flops | bytes accessed | tf_op | source)
XLA Modules:
  0.0 219.6 jit_solution(4436296063921358149)
XLA Ops:
  6.2 5.9 %collective-permute-start.1 = (f32[8,8,128]{2,1,0:T(8,128)S(1)}, f32[8,8,128]{2,1,0:T(8,128)S(1)}, u32[]{:S(2)}, u32[]{:S(2)}) collective-permute-start(f32[8,8,128]{2,1,0:T(8,128)S(1)} %fusion.6), channel_id=1, source_target_pairs={{0,7},{16,23},{32,39},{48,55},{64,71},{80,87},{96,103},{112,119},{... | collective-permute-start | bytes 98312 | tf_op jit(solution)/shard_map/ppermute | solution.py:30
  14.1 3.9 %collective-permute-start.3 = (f32[2,64,64]{2,1,0:T(8,128)S(1)}, f32[2,64,64]{2,1,0:T(8,128)S(1)}, u32[]{:S(2)}, u32[]{:S(2)}) collective-permute-start(f32[2,64,64]{2,1,0:T(8,128)S(1)} %copy-done.3), channel_id=1, source_target_pairs={{0,1},{1,2},{2,3},{3,4},{4,5},{5,6},{6,7},{7,8},{8,9},{9,10},{10,1... | collective-permute-start | bytes 98312 | tf_op jit(solution)/shard_map/ppermute | solution.py:249
  18.3 5.9 %collective-permute-done.3 = f32[2,64,64]{2,1,0:T(8,128)S(1)} collective-permute-done((f32[2,64,64]{2,1,0:T(8,128)S(1)}, f32[2,64,64]{2,1,0:T(8,128)S(1)}, u32[]{:S(2)}, u32[]{:S(2)}) %collective-permute-start.3) | collective-permute-done | bytes 32800 | tf_op jit(solution)/shard_map/ppermute | solution.py:249
  24.3 5.1 %collective-permute-done.5 = f32[8,8,128]{2,1,0:T(8,128)S(1)} collective-permute-done((f32[8,8,128]{2,1,0:T(8,128)S(1)}, f32[8,8,128]{2,1,0:T(8,128)S(1)}, u32[]{:S(2)}, u32[]{:S(2)}) %collective-permute-start.5) | collective-permute-done | bytes 32800 | tf_op jit(solution)/shard_map/ppermute | solution.py:30
  32.5 3.0 %collective-permute-start.8 = (f32[2,192,64]{2,1,0:T(8,128)S(1)}, f32[2,192,64]{2,1,0:T(8,128)S(1)}, u32[]{:S(2)}, u32[]{:S(2)}) collective-permute-start(f32[2,192,64]{2,1,0:T(8,128)S(1)} %pad_maximum_fusion.2), channel_id=1, source_target_pairs={{0,16},{16,32},{32,48},{48,64},{64,80},{80,96},{96,112},{112,128},... | collective-permute-start | bytes 294920 | tf_op jit(solution)/shard_map/ppermute | solution.py:249
  37.9 3.2 %collective-permute-done.7 = f32[2,8,8,128]{3,2,1,0:T(8,128)S(1)} collective-permute-done((f32[2,8,8,128]{3,2,1,0:T(8,128)S(1)}, f32[2,8,8,128]{3,2,1,0:T(8,128)S(1)}, u32[]{:S(2)}, u32[]{:S(2)}) %collective-permute-start.7) | collective-permute-done | bytes 65568 | tf_op jit(solution)/shard_map/ppermute | solution.py:30
  43.2 3.0 %collective-permute-done.10 = f32[4,8,8,128]{3,2,1,0:T(8,128)S(1)} collective-permute-done((f32[4,8,8,128]{3,2,1,0:T(8,128)S(1)}, f32[4,8,8,128]{3,2,1,0:T(8,128)S(1)}, u32[]{:S(2)}, u32[]{:S(2)}) %collective-permute-start.10) | collective-permute-done | bytes 131104 | tf_op jit(solution)/shard_map/ppermute | solution.py:30
  46.4 6.3 %collective-permute-done.11 = f32[8,8,8,128]{3,2,1,0:T(8,128)S(1)} collective-permute-done((f32[8,8,8,128]{3,2,1,0:T(8,128)S(1)}, f32[8,8,8,128]{3,2,1,0:T(8,128)S(1)}, u32[]{:S(2)}, u32[]{:S(2)}) %collective-permute-start.11) | collective-permute-done | bytes 262176 | tf_op jit(solution)/shard_map/ppermute | solution.py:30
  54.7 15.5 %sweep.2 = (f32[16,9,8,128]{3,2,1,0:T(8,128)S(1)}, f32[16,9,8,128]{3,2,1,0:T(8,128)S(1)}, f32[3,64,256]{2,1,0:T(8,128)S(1)}, f32[3,64,256]{2,1,0:T(8,128)S(1)}, f32[3,64,256]{2,1,0:T(8,128)S(1)}) custom-call(s32[12,2]{1,0:T(8,128)S(1)} %copy.8.pos_ref, s32[3]{0:T(128)S(1)} %pad_add_fusion.spot_ref, f32[2,192,256]{2,1,0:T(8,128)S(1)} %maximum_maximum_fusion.ext_ref, ...), custom_call_target="tpu_custom_call" | custom-call | flops 6442450944 | bytes 8388608 | tf_op jit(solution)/shard_map/sweep/pallas_call | solution.py:223
  74.4 7.5 %collective-permute-start.17 = (f32[3,64,256]{2,1,0:T(8,128)S(1)}, f32[3,64,256]{2,1,0:T(8,128)S(1)}, u32[]{:S(2)}, u32[]{:S(2)}) collective-permute-start(f32[3,64,256]{2,1,0:T(8,128)S(1)} %get-tuple-element.48), channel_id=1, source_target_pairs={{1,0},{2,1},{3,2},{4,3},{5,4},{6,5},{7,6},{8,7},{9,8},{10,9},{11,1... | collective-permute-start | bytes 589832 | tf_op jit(solution)/shard_map/ppermute | solution.py:249
  82.0 3.2 %collective-permute-start.15 = (f32[4,9,8,128]{3,2,1,0:T(8,128)S(1)}, f32[4,9,8,128]{3,2,1,0:T(8,128)S(1)}, u32[]{:S(2)}, u32[]{:S(2)}) collective-permute-start(f32[4,9,8,128]{3,2,1,0:T(8,128)S(1)} %slice.121), channel_id=1, source_target_pairs={{0,32},{16,80},{32,0},{48,112},{64,96},{80,16},{96,64},{112,48},{1... | collective-permute-start | bytes 442376 | tf_op jit(solution)/shard_map/ppermute | solution.py:30
  94.1 3.0 %collective-permute-start.19 = (f32[1,9,8,128]{3,2,1,0:T(8,128)S(1)}, f32[1,9,8,128]{3,2,1,0:T(8,128)S(1)}, u32[]{:S(2)}, u32[]{:S(2)}) collective-permute-start(f32[1,9,8,128]{3,2,1,0:T(8,128)S(1)} %slice.123), channel_id=1, source_target_pairs={{0,64},{16,48},{32,96},{48,16},{64,0},{80,112},{96,32},{112,80},{1... | collective-permute-start | bytes 110600 | tf_op jit(solution)/shard_map/ppermute | solution.py:30
  100.3 7.0 %collective-permute-start.25 = (f32[2,64,64]{2,1,0:T(8,128)S(1)}, f32[2,64,64]{2,1,0:T(8,128)S(1)}, u32[]{:S(2)}, u32[]{:S(2)}) collective-permute-start(f32[2,64,64]{2,1,0:T(8,128)S(1)} %divide_subtract_fusion.1), channel_id=1, source_target_pairs={{1,0},{2,1},{3,2},{4,3},{5,4},{6,5},{7,6},{8,7},{9,8},{10,9},{11,1... | collective-permute-start | bytes 98312 | tf_op jit(solution)/shard_map/ppermute | solution.py:249
  109.8 8.0 %collective-permute-done.24 = f32[2,64,64]{2,1,0:T(8,128)S(1)} collective-permute-done((f32[2,64,64]{2,1,0:T(8,128)S(1)}, f32[2,64,64]{2,1,0:T(8,128)S(1)}, u32[]{:S(2)}, u32[]{:S(2)}) %collective-permute-start.24) | collective-permute-done | bytes 32800 | tf_op jit(solution)/shard_map/ppermute | solution.py:249
  119.1 3.0 %collective-permute-start.27 = (f32[2,192,64]{2,1,0:T(8,128)S(1)}, f32[2,192,64]{2,1,0:T(8,128)S(1)}, u32[]{:S(2)}, u32[]{:S(2)}) collective-permute-start(f32[2,192,64]{2,1,0:T(8,128)S(1)} %pad_maximum_fusion.3), channel_id=1, source_target_pairs={{0,16},{16,32},{32,48},{48,64},{64,80},{80,96},{96,112},{112,128},... | collective-permute-start | bytes 294920 | tf_op jit(solution)/shard_map/ppermute | solution.py:249
  126.2 5.5 %collective-permute-done.29 = f32[9,8,128]{2,1,0:T(8,128)S(1)} collective-permute-done((f32[9,8,128]{2,1,0:T(8,128)S(1)}, f32[9,8,128]{2,1,0:T(8,128)S(1)}, u32[]{:S(2)}, u32[]{:S(2)}) %collective-permute-start.29) | collective-permute-done | bytes 36896 | tf_op jit(solution)/shard_map/ppermute | solution.py:30
  138.2 3.8 %collective-permute-done.31 = f32[2,8,8,128]{3,2,1,0:T(8,128)S(1)} collective-permute-done((f32[2,8,8,128]{3,2,1,0:T(8,128)S(1)}, f32[2,8,8,128]{3,2,1,0:T(8,128)S(1)}, u32[]{:S(2)}, u32[]{:S(2)}) %collective-permute-start.31) | collective-permute-done | bytes 65568 | tf_op jit(solution)/shard_map/ppermute | solution.py:30
  148.2 5.5 %collective-permute-done.33 = f32[8,8,8,128]{3,2,1,0:T(8,128)S(1)} collective-permute-done((f32[8,8,8,128]{3,2,1,0:T(8,128)S(1)}, f32[8,8,8,128]{3,2,1,0:T(8,128)S(1)}, u32[]{:S(2)}, u32[]{:S(2)}) %collective-permute-start.33) | collective-permute-done | bytes 262176 | tf_op jit(solution)/shard_map/ppermute | solution.py:30
  155.7 15.5 %sweep.3 = (f32[16,9,8,128]{3,2,1,0:T(8,128)S(1)}, f32[16,9,8,128]{3,2,1,0:T(8,128)S(1)}, f32[3,64,256]{2,1,0:T(8,128)S(1)}, f32[3,64,256]{2,1,0:T(8,128)S(1)}, f32[3,64,256]{2,1,0:T(8,128)S(1)}) custom-call(s32[12,2]{1,0:T(8,128)S(1)} %copy.8.pos_ref, s32[3]{0:T(128)S(1)} %pad_add_fusion.spot_ref, f32[2,192,256]{2,1,0:T(8,128)S(1)} %maximum_maximum_fusion.1.ext_ref, ...), custom_call_target="tpu_custom_call" | custom-call | flops 6442450944 | bytes 8388608 | tf_op jit(solution)/shard_map/sweep/pallas_call | solution.py:223
  176.3 7.5 %collective-permute-start.39 = (f32[3,64,256]{2,1,0:T(8,128)S(1)}, f32[3,64,256]{2,1,0:T(8,128)S(1)}, u32[]{:S(2)}, u32[]{:S(2)}) collective-permute-start(f32[3,64,256]{2,1,0:T(8,128)S(1)} %get-tuple-element.65), channel_id=1, source_target_pairs={{1,0},{2,1},{3,2},{4,3},{5,4},{6,5},{7,6},{8,7},{9,8},{10,9},{11,1... | collective-permute-start | bytes 589832 | tf_op jit(solution)/shard_map/ppermute | solution.py:249
  199.5 3.9 %collective-permute-done.44 = f32[9,8,128]{2,1,0:T(8,128)S(1)} collective-permute-done((f32[9,8,128]{2,1,0:T(8,128)S(1)}, f32[9,8,128]{2,1,0:T(8,128)S(1)}, u32[]{:S(2)}, u32[]{:S(2)}) %collective-permute-start.44) | collective-permute-done | bytes 36896 | tf_op jit(solution)/shard_map/ppermute | solution.py:30
  203.5 4.4 %collective-permute-start.45 = (f32[9,8,128]{2,1,0:T(8,128)S(1)}, f32[9,8,128]{2,1,0:T(8,128)S(1)}, u32[]{:S(2)}, u32[]{:S(2)}) collective-permute-start(f32[9,8,128]{2,1,0:T(8,128)S(1)} %add.163), channel_id=1, source_target_pairs={{0,7},{16,23},{32,39},{48,55},{64,71},{80,87},{96,103},{112,119},{... | collective-permute-start | bytes 110600 | tf_op jit(solution)/shard_map/ppermute | solution.py:30
  209.8 3.9 %collective-permute-done.46 = f32[9,8,128]{2,1,0:T(8,128)S(1)} collective-permute-done((f32[9,8,128]{2,1,0:T(8,128)S(1)}, f32[9,8,128]{2,1,0:T(8,128)S(1)}, u32[]{:S(2)}, u32[]{:S(2)}) %collective-permute-start.46) | collective-permute-done | bytes 36896 | tf_op jit(solution)/shard_map/ppermute | solution.py:30
  213.7 3.2 %collective-permute-start.47 = (f32[9,8,128]{2,1,0:T(8,128)S(1)}, f32[9,8,128]{2,1,0:T(8,128)S(1)}, u32[]{:S(2)}, u32[]{:S(2)}) collective-permute-start(f32[9,8,128]{2,1,0:T(8,128)S(1)} %collective-permute-done.46), channel_id=1, source_target_pairs={{0,7},{16,23},{32,39},{48,55},{64,71},{80,87},{96,103},{112,119},{... | collective-permute-start | bytes 110600 | tf_op jit(solution)/shard_map/ppermute | solution.py:30
  (149 shorter events, 81.4 us)
Async XLA Ops:
  6.2 11.8 %collective-permute-start.1 = (f32[8,8,128]{2,1,0:T(8,128)S(1)}, f32[8,8,128]{2,1,0:T(8,128)S(1)}, u32[]{:S(2)}, u32[]{:S(2)}) collective-permute-start(f32[8,8,128]{2,1,0:T(8,128)S(1)} %fusion.6), channel_id=1, source_target_pairs={{0,7},{16,23},{32,39},{48,55},{64,71},{80,87},{96,103},{112,119},{... | collective-permute-start | bytes 98312 | tf_op jit(solution)/shard_map/ppermute | solution.py:30
  12.2 6.1 %collective-permute-start.4 = (f32[2,64,64]{2,1,0:T(8,128)S(1)}, f32[2,64,64]{2,1,0:T(8,128)S(1)}, u32[]{:S(2)}, u32[]{:S(2)}) collective-permute-start(f32[2,64,64]{2,1,0:T(8,128)S(1)} %copy-done.3), channel_id=1, source_target_pairs={{1,0},{2,1},{3,2},{4,3},{5,4},{6,5},{7,6},{8,7},{9,8},{10,9},{11,1... | collective-permute-start | bytes 98312 | tf_op jit(solution)/shard_map/ppermute | solution.py:249
  14.1 10.1 %collective-permute-start.3 = (f32[2,64,64]{2,1,0:T(8,128)S(1)}, f32[2,64,64]{2,1,0:T(8,128)S(1)}, u32[]{:S(2)}, u32[]{:S(2)}) collective-permute-start(f32[2,64,64]{2,1,0:T(8,128)S(1)} %copy-done.3), channel_id=1, source_target_pairs={{0,1},{1,2},{2,3},{3,4},{4,5},{5,6},{6,7},{7,8},{8,9},{9,10},{10,1... | collective-permute-start | bytes 98312 | tf_op jit(solution)/shard_map/ppermute | solution.py:249
  18.0 6.2 %collective-permute-start.2 = (f32[8,8,128]{2,1,0:T(8,128)S(1)}, f32[8,8,128]{2,1,0:T(8,128)S(1)}, u32[]{:S(2)}, u32[]{:S(2)}) collective-permute-start(f32[8,8,128]{2,1,0:T(8,128)S(1)} %collective-permute-done.1), channel_id=1, source_target_pairs={{0,1},{16,17},{32,33},{48,49},{64,65},{80,81},{96,97},{112,113},{1... | collective-permute-start | bytes 98312 | tf_op jit(solution)/shard_map/ppermute | solution.py:30
  29.5 6.0 %collective-permute-start.6 = (f32[1,8,8,128]{3,2,1,0:T(8,128)S(1)}, f32[1,8,8,128]{3,2,1,0:T(8,128)S(1)}, u32[]{:S(2)}, u32[]{:S(2)}) collective-permute-start(f32[1,8,8,128]{3,2,1,0:T(8,128)S(1)} %bitcast.34), channel_id=1, source_target_pairs={{0,64},{16,48},{32,96},{48,16},{64,0},{80,112},{96,32},{112,80},{1... | collective-permute-start | bytes 98312 | tf_op jit(solution)/shard_map/ppermute | solution.py:30
  31.2 6.5 %collective-permute-start.9 = (f32[2,192,64]{2,1,0:T(8,128)S(1)}, f32[2,192,64]{2,1,0:T(8,128)S(1)}, u32[]{:S(2)}, u32[]{:S(2)}) collective-permute-start(f32[2,192,64]{2,1,0:T(8,128)S(1)} %pad_maximum_fusion.2), channel_id=1, source_target_pairs={{16,0},{32,16},{48,32},{64,48},{80,64},{96,80},{112,96},{128,112},... | collective-permute-start | bytes 294920 | tf_op jit(solution)/shard_map/ppermute | solution.py:249
  46.2 6.5 %collective-permute-start.11 = (f32[8,8,8,128]{3,2,1,0:T(8,128)S(1)}, f32[8,8,8,128]{3,2,1,0:T(8,128)S(1)}, u32[]{:S(2)}, u32[]{:S(2)}) collective-permute-start(f32[8,8,8,128]{3,2,1,0:T(8,128)S(1)} %pad_maximum_fusion), channel_id=1, source_target_pairs={{0,40},{16,208},{32,8},{48,240},{64,104},{80,144},{96,72},{112,176... | collective-permute-start | bytes 786440 | tf_op jit(solution)/shard_map/ppermute | solution.py:30
  72.4 9.6 %collective-permute-start.14 = (f32[8,9,8,128]{3,2,1,0:T(8,128)S(1)}, f32[8,9,8,128]{3,2,1,0:T(8,128)S(1)}, u32[]{:S(2)}, u32[]{:S(2)}) collective-permute-start(f32[8,9,8,128]{3,2,1,0:T(8,128)S(1)} %slice.91), channel_id=1, source_target_pairs={{0,40},{16,208},{32,8},{48,240},{64,104},{80,144},{96,72},{112,176... | collective-permute-start | bytes 884744 | tf_op jit(solution)/shard_map/ppermute | solution.py:30
  72.5 12.8 %collective-permute-start.16 = (f32[3,64,256]{2,1,0:T(8,128)S(1)}, f32[3,64,256]{2,1,0:T(8,128)S(1)}, u32[]{:S(2)}, u32[]{:S(2)}) collective-permute-start(f32[3,64,256]{2,1,0:T(8,128)S(1)} %get-tuple-element.47), channel_id=1, source_target_pairs={{0,1},{1,2},{2,3},{3,4},{4,5},{5,6},{6,7},{7,8},{8,9},{9,10},{10,1... | collective-permute-start | bytes 589832 | tf_op jit(solution)/shard_map/ppermute | solution.py:249
  74.4 12.0 %collective-permute-start.17 = (f32[3,64,256]{2,1,0:T(8,128)S(1)}, f32[3,64,256]{2,1,0:T(8,128)S(1)}, u32[]{:S(2)}, u32[]{:S(2)}) collective-permute-start(f32[3,64,256]{2,1,0:T(8,128)S(1)} %get-tuple-element.48), channel_id=1, source_target_pairs={{1,0},{2,1},{3,2},{4,3},{5,4},{6,5},{7,6},{8,7},{9,8},{10,9},{11,1... | collective-permute-start | bytes 589832 | tf_op jit(solution)/shard_map/ppermute | solution.py:249
  82.0 6.4 %collective-permute-start.15 = (f32[4,9,8,128]{3,2,1,0:T(8,128)S(1)}, f32[4,9,8,128]{3,2,1,0:T(8,128)S(1)}, u32[]{:S(2)}, u32[]{:S(2)}) collective-permute-start(f32[4,9,8,128]{3,2,1,0:T(8,128)S(1)} %slice.121), channel_id=1, source_target_pairs={{0,32},{16,80},{32,0},{48,112},{64,96},{80,16},{96,64},{112,48},{1... | collective-permute-start | bytes 442376 | tf_op jit(solution)/shard_map/ppermute | solution.py:30
  88.5 5.7 %collective-permute-start.18 = (f32[2,9,8,128]{3,2,1,0:T(8,128)S(1)}, f32[2,9,8,128]{3,2,1,0:T(8,128)S(1)}, u32[]{:S(2)}, u32[]{:S(2)}) collective-permute-start(f32[2,9,8,128]{3,2,1,0:T(8,128)S(1)} %slice.95), channel_id=1, source_target_pairs={{0,192},{16,56},{32,224},{48,24},{64,128},{80,120},{96,160},{112,8... | collective-permute-start | bytes 221192 | tf_op jit(solution)/shard_map/ppermute | solution.py:30
  90.7 6.4 %collective-permute-start.20 = (f32[3,64,64]{2,1,0:T(8,128)S(1)}, f32[3,64,64]{2,1,0:T(8,128)S(1)}, u32[]{:S(2)}, u32[]{:S(2)}) collective-permute-start(f32[3,64,64]{2,1,0:T(8,128)S(1)} %get-tuple-element.72), channel_id=1, source_target_pairs={{0,16},{16,32},{32,48},{48,64},{64,80},{80,96},{96,112},{112,128},... | collective-permute-start | bytes 147464 | tf_op jit(solution)/shard_map/ppermute | solution.py:249
  94.1 5.8 %collective-permute-start.19 = (f32[1,9,8,128]{3,2,1,0:T(8,128)S(1)}, f32[1,9,8,128]{3,2,1,0:T(8,128)S(1)}, u32[]{:S(2)}, u32[]{:S(2)}) collective-permute-start(f32[1,9,8,128]{3,2,1,0:T(8,128)S(1)} %slice.123), channel_id=1, source_target_pairs={{0,64},{16,48},{32,96},{48,16},{64,0},{80,112},{96,32},{112,80},{1... | collective-permute-start | bytes 110600 | tf_op jit(solution)/shard_map/ppermute | solution.py:30
  100.0 9.3 %collective-permute-start.22 = (f32[9,8,128]{2,1,0:T(8,128)S(1)}, f32[9,8,128]{2,1,0:T(8,128)S(1)}, u32[]{:S(2)}, u32[]{:S(2)}) collective-permute-start(f32[9,8,128]{2,1,0:T(8,128)S(1)} %fusion.1), channel_id=1, source_target_pairs={{0,1},{16,17},{32,33},{48,49},{64,65},{80,81},{96,97},{112,113},{1... | collective-permute-start | bytes 110600 | tf_op jit(solution)/shard_map/ppermute | solution.py:30
  100.3 9.5 %collective-permute-start.25 = (f32[2,64,64]{2,1,0:T(8,128)S(1)}, f32[2,64,64]{2,1,0:T(8,128)S(1)}, u32[]{:S(2)}, u32[]{:S(2)}) collective-permute-start(f32[2,64,64]{2,1,0:T(8,128)S(1)} %divide_subtract_fusion.1), channel_id=1, source_target_pairs={{1,0},{2,1},{3,2},{4,3},{5,4},{6,5},{7,6},{8,7},{9,8},{10,9},{11,1... | collective-permute-start | bytes 98312 | tf_op jit(solution)/shard_map/ppermute | solution.py:249
  107.3 10.5 %collective-permute-start.24 = (f32[2,64,64]{2,1,0:T(8,128)S(1)}, f32[2,64,64]{2,1,0:T(8,128)S(1)}, u32[]{:S(2)}, u32[]{:S(2)}) collective-permute-start(f32[2,64,64]{2,1,0:T(8,128)S(1)} %divide_subtract_fusion.1), channel_id=1, source_target_pairs={{0,1},{1,2},{2,3},{3,4},{4,5},{5,6},{6,7},{7,8},{8,9},{9,10},{10,1... | collective-permute-start | bytes 98312 | tf_op jit(solution)/shard_map/ppermute | solution.py:249
  109.3 8.5 %collective-permute-start.23 = (f32[9,8,128]{2,1,0:T(8,128)S(1)}, f32[9,8,128]{2,1,0:T(8,128)S(1)}, u32[]{:S(2)}, u32[]{:S(2)}) collective-permute-start(f32[9,8,128]{2,1,0:T(8,128)S(1)} %add.146), channel_id=1, source_target_pairs={{0,7},{16,23},{32,39},{48,55},{64,71},{80,87},{96,103},{112,119},{... | collective-permute-start | bytes 110600 | tf_op jit(solution)/shard_map/ppermute | solution.py:30
  147.2 6.5 %collective-permute-start.33 = (f32[8,8,8,128]{3,2,1,0:T(8,128)S(1)}, f32[8,8,8,128]{3,2,1,0:T(8,128)S(1)}, u32[]{:S(2)}, u32[]{:S(2)}) collective-permute-start(f32[8,8,8,128]{3,2,1,0:T(8,128)S(1)} %pad_maximum_fusion.1), channel_id=1, source_target_pairs={{0,40},{16,208},{32,8},{48,240},{64,104},{80,144},{96,72},{112,176... | collective-permute-start | bytes 786440 | tf_op jit(solution)/shard_map/ppermute | solution.py:30
  173.4 10.4 %collective-permute-start.36 = (f32[8,9,8,128]{3,2,1,0:T(8,128)S(1)}, f32[8,9,8,128]{3,2,1,0:T(8,128)S(1)}, u32[]{:S(2)}, u32[]{:S(2)}) collective-permute-start(f32[8,9,8,128]{3,2,1,0:T(8,128)S(1)} %slice.106), channel_id=1, source_target_pairs={{0,40},{16,208},{32,8},{48,240},{64,104},{80,144},{96,72},{112,176... | collective-permute-start | bytes 884744 | tf_op jit(solution)/shard_map/ppermute | solution.py:30
  174.3 13.0 %collective-permute-start.38 = (f32[3,64,256]{2,1,0:T(8,128)S(1)}, f32[3,64,256]{2,1,0:T(8,128)S(1)}, u32[]{:S(2)}, u32[]{:S(2)}) collective-permute-start(f32[3,64,256]{2,1,0:T(8,128)S(1)} %get-tuple-element.64), channel_id=1, source_target_pairs={{0,1},{1,2},{2,3},{3,4},{4,5},{5,6},{6,7},{7,8},{8,9},{9,10},{10,1... | collective-permute-start | bytes 589832 | tf_op jit(solution)/shard_map/ppermute | solution.py:249
  176.3 12.2 %collective-permute-start.39 = (f32[3,64,256]{2,1,0:T(8,128)S(1)}, f32[3,64,256]{2,1,0:T(8,128)S(1)}, u32[]{:S(2)}, u32[]{:S(2)}) collective-permute-start(f32[3,64,256]{2,1,0:T(8,128)S(1)} %get-tuple-element.65), channel_id=1, source_target_pairs={{1,0},{2,1},{3,2},{4,3},{5,4},{6,5},{7,6},{8,7},{9,8},{10,9},{11,1... | collective-permute-start | bytes 589832 | tf_op jit(solution)/shard_map/ppermute | solution.py:249
  189.5 5.7 %collective-permute-start.40 = (f32[2,9,8,128]{3,2,1,0:T(8,128)S(1)}, f32[2,9,8,128]{3,2,1,0:T(8,128)S(1)}, u32[]{:S(2)}, u32[]{:S(2)}) collective-permute-start(f32[2,9,8,128]{3,2,1,0:T(8,128)S(1)} %slice.110), channel_id=1, source_target_pairs={{0,192},{16,56},{32,224},{48,24},{64,128},{80,120},{96,160},{112,8... | collective-permute-start | bytes 221192 | tf_op jit(solution)/shard_map/ppermute | solution.py:30
  203.5 6.3 %collective-permute-start.45 = (f32[9,8,128]{2,1,0:T(8,128)S(1)}, f32[9,8,128]{2,1,0:T(8,128)S(1)}, u32[]{:S(2)}, u32[]{:S(2)}) collective-permute-start(f32[9,8,128]{2,1,0:T(8,128)S(1)} %add.163), channel_id=1, source_target_pairs={{0,7},{16,23},{32,39},{48,55},{64,71},{80,87},{96,103},{112,119},{... | collective-permute-start | bytes 110600 | tf_op jit(solution)/shard_map/ppermute | solution.py:30
  (30 other events, 171.9 us)
